TPU v7x, 32 devices: a whole 2x2x4 slice. The times are simulated.
32 devices in a mesh: grp: 4 (over z), wide: 8 (over y, x, core).
Axes of the slice: x: 2, y: 2, z: 4, core: 2. Of those that a mesh axis runs over, the one named last changes fastest.
Arguments:
- a_vals: bfloat16 [1024, 7, 128, 128], P(('grp', 'wide')), may hold values from -0.5 to 0.5
- a_cols: int32 [1024, 7], P(('grp', 'wide')), may hold values from 0 to 1023, as said below
- p_vals: bfloat16 [1024, 128, 128], P(('grp', 'wide')), may hold values from -1.75 to 1.75
- tile_slot: int32 [1024, 7], P(('grp', 'wide')), may hold values from 0 to 2047, as said below
Outputs:
- coarse: float32 [2048, 128, 128], P(('grp', 'wide'))
Inputs may be any that keep to these rules, and one draw needn't show every extreme that they name: `a_cols`: entry 0 of fine block row i is i itself; every entry j satisfies (j // 32) % 8 = (i // 32) % 8. `tile_slot`: the 7 entries of a fine block row name different slots of one coarse block row, all below the same multiple of 8; the slot's device s // 64 has the same grp index (s // 64) // 8 as the row's device (i // 32) // 8. The fine block rows of one device send to one device at most 8 rows; in every draw some device receives exactly 8 rows from every device of its grp index.
All inputs are finite; a program needn't handle non-finite values.
Results may differ from a plain program's by a relative error of at most 0.005.
Values may be sent and summed in bfloat16 or wider, within the bound.
No kernel may reach another device: no remote copies, remote signals or barrier semaphores. Data moves between devices by JAX's collectives and lax.ppermute only.
A program may use at most 192 MiB of HBM per device.

v0:
```python
import jax
import jax.numpy as jnp
from jax import lax
from jax.sharding import PartitionSpec as P

SLOT_DEV = 64


def on_device(a_vals, a_cols, p_vals, tile_slot):
    local_rows = a_vals.shape[0]
    per_row = a_vals.shape[1]
    block_side = a_vals.shape[2]
    owners = lax.axis_size("wide")
    capacity = max(2, (2 * local_rows + owners - 1) // owners)
    gathered = lax.all_gather(p_vals, "grp", axis=0, tiled=True)
    source_plane = a_cols // (owners * local_rows)
    offset = a_cols % local_rows
    picked = gathered[source_plane * local_rows + offset]
    products = jnp.einsum(
        "rkab,rkbc->rkac", a_vals, picked, preferred_element_type=jnp.float32
    ).astype(jnp.bfloat16)
    target = tile_slot[:, 0] // SLOT_DEV % owners
    owner_marks = (target[:, None] == jnp.arange(owners, dtype=jnp.int32)[None, :]).astype(
        jnp.int32
    )
    before = jnp.cumsum(owner_marks, axis=0) - owner_marks
    rank_in = jnp.sum(before * owner_marks, axis=1)
    position = target * capacity + rank_in
    local_slot = (tile_slot % SLOT_DEV).astype(jnp.float32)
    empty_slot = jnp.full((owners * capacity, per_row), float(SLOT_DEV), jnp.float32)
    slot_buffer = empty_slot.at[position].set(local_slot).astype(jnp.bfloat16)
    own_buffer = (
        jnp.zeros((owners * capacity, block_side, block_side), jnp.bfloat16)
        .at[position]
        .set(p_vals)
    )
    factor_buffer = (
        jnp.zeros((owners * capacity, per_row, block_side, block_side), jnp.bfloat16)
        .at[position]
        .set(products)
    )
    got_rows, got_factors, got_slots = (
        lax.all_to_all(own_buffer, "wide", split_axis=0, concat_axis=0, tiled=True),
        lax.all_to_all(factor_buffer, "wide", split_axis=0, concat_axis=0, tiled=True),
        lax.all_to_all(slot_buffer, "wide", split_axis=0, concat_axis=0, tiled=True),
    )
    got_tiles = jnp.einsum(
        "rab,rkac->rkbc", got_rows, got_factors, preferred_element_type=jnp.float32
    ).astype(jnp.bfloat16)
    target_index = got_slots.astype(jnp.int32).reshape(-1)
    coarse = jnp.zeros((SLOT_DEV, block_side, block_side), jnp.float32)
    coarse = coarse.at[target_index].add(
        got_tiles.astype(jnp.float32).reshape(-1, block_side, block_side), mode="drop"
    )
    return coarse


def solution(mesh):
    placed = (
        P(("grp", "wide"), None, None, None),
        P(("grp", "wide"), None),
        P(("grp", "wide"), None, None),
        P(("grp", "wide"), None),
    )
    return jax.shard_map(
        on_device,
        mesh=mesh,
        in_specs=placed,
        out_specs=P(("grp", "wide"), None, None),
        check_vma=False,
    )
```

profile of v0, /device:TPU:3, one launch (start us, length us, event | category | flops | bytes accessed | tf_op | source)
XLA Modules:
  0.0 484.4 jit_solution(16952469553419013228)
XLA Ops:
  6.5 0.7 all-gather.2.cloned.1.call-update
  7.3 0.7 fusion.5
  8.0 0.7 fusion.16
  8.9 0.2 select_reduce_fusion
  9.1 0.7 fusion.12
  9.8 0.7 scatter_custom_fusion
  10.5 0.6 convert_bitcast_fusion.1
  11.1 4.5 all-to-all-start
  15.6 1.8 broadcast_in_dim.25
  17.4 5.5 %scatter_fusion.1 = bf16[64,128,128]{2,1,0:T(8,128)(2,1)} fusion(bf16[64,128,128]{2,1,0:T(8,128)(2,1)} %broadcast_in_dim.25, s32[32]{0:T(128)S(1)} %fusion.12, bf16[32,128,128]{2,1,0:T(8,128)(2,1)} %param.6), kind=kCustom, calls=%fused_computation.3 | custom fusion | bytes 3145856 | tf_op jit(solution)/shard_map/scatter | solution.py:35
  22.9 4.2 all-to-all-start.2
  27.4 63.4 %all-gather.2.cloned.1.call-done = bf16[128,128,128]{2,1,0:T(8,128)(2,1)} async-done(((bf16[32,128,128]{2,1,0:T(8,128)(2,1)}), bf16[128,128,128]{2,1,0:T(8,128)(2,1)}) %all-gather.2.cloned.1.call-update) | async-done | bytes 4194320 | tf_op jit(solution)/shard_map/all_gather | solution.py:15
  90.8 10.6 %gather_fusion = bf16[224,128,128]{2,1,0:T(8,128)(2,1)} fusion(bf16[128,128,128]{2,1,0:T(8,128)(2,1)} %all-gather.2.cloned.1.call-done, s32[1024]{0:T(1024)S(1)} %pad_clamp_fusion), kind=kCustom, calls=%fused_computation | custom fusion | bytes 14680960 | tf_op jit(solution)/shard_map/gather | solution.py:18
  101.3 10.5 %convert_bitcast_fusion = bf16[32,7,128,128]{2,3,1,0:T(8,128)(2,1)} fusion(bf16[32,7,128,128]{3,2,1,0:T(8,128)(2,1)} %bitcast.26, bf16[32,7,128,128]{3,2,1,0:T(8,128)(2,1)} %param.4), kind=kOutput, calls=%fused_computation.6 | convolution fusion | flops 943194112 | bytes 22020096 | tf_op jit(solution)/shard_map/rkab,rkbc->rkac/dot_general | solution.py:19
  111.8 10.7 %copy.14 = bf16[32,7,128,128]{3,2,1,0:T(8,128)(2,1)} copy(bf16[32,7,128,128]{2,3,1,0:T(8,128)(2,1)} %convert_bitcast_fusion) | data formatting | bytes 14680064 | tf_op jit(solution)/shard_map/convert_element_type | solution.py:21
  122.5 9.0 %broadcast_in_dim.23 = bf16[64,7,128,128]{3,2,1,0:T(8,128)(2,1)} broadcast(bf16[]{:T(256)} %constant.81.clone.1), dimensions={} | broadcast | bytes 14680066 | tf_op jit(solution)/shard_map/broadcast_in_dim | solution.py:38
  131.5 21.3 %scatter_fusion = bf16[64,7,128,128]{3,2,1,0:T(8,128)(2,1)} fusion(bf16[64,7,128,128]{3,2,1,0:T(8,128)(2,1)} %broadcast_in_dim.23, s32[32]{0:T(128)S(1)} %fusion.12, bf16[32,7,128,128]{3,2,1,0:T(8,128)(2,1)} %copy.14), kind=kCustom, calls=%fused_computation.2 | custom fusion | bytes 22020224 | tf_op jit(solution)/shard_map/scatter | solution.py:40
  152.8 20.7 %copy.15 = bf16[64,7,128,128]{2,3,1,0:T(8,128)(2,1)} copy(bf16[64,7,128,128]{3,2,1,0:T(8,128)(2,1)} %scatter_fusion) | data formatting | bytes 29360128 | tf_op jit(solution)/shard_map/scatter | solution.py:40
  173.5 6.5 %all-to-all-start.1 = ((bf16[64,7,128,128]{2,3,1,0:T(8,128)(2,1)}), bf16[64,7,128,128]{2,3,1,0:T(8,128)(2,1)}, u32[]{:S(2)}, u32[]{:S(2)}) async-start(bf16[64,7,128,128]{2,3,1,0:T(8,128)(2,1)} %copy.15), calls=%async_computation.1 | async-start | bytes 29360128 | tf_op jit(solution)/shard_map/all_to_all | solution.py:44
  180.1 159.8 %all-to-all-done.1 = bf16[64,7,128,128]{2,3,1,0:T(8,128)(2,1)} async-done(((bf16[64,7,128,128]{2,3,1,0:T(8,128)(2,1)}), bf16[64,7,128,128]{2,3,1,0:T(8,128)(2,1)}, u32[]{:S(2)}, u32[]{:S(2)}) %all-to-all-start.1) | async-done | bytes 14680096 | tf_op jit(solution)/shard_map/all_to_all | solution.py:44
  340.0 14.7 %convert_convert_fusion = f32[64,7,128,128]{3,2,1,0:T(8,128)} fusion(bf16[64,7,128,128]{2,3,1,0:T(8,128)(2,1)} %all-to-all-done.1, bf16[64,128,128]{2,1,0:T(8,128)(2,1)S(1)} %all-to-all-done.2), kind=kOutput, calls=%fused_computation.5 | convolution fusion | flops 1893728256 | bytes 46137344 | tf_op jit(solution)/shard_map/rab,rkac->rkbc/dot_general | solution.py:47
  354.7 29.5 %copy.16 = f32[448,128,128]{2,1,0:T(8,128)} copy(f32[448,128,128]{1,2,0:T(8,128)} %bitcast.25) | data formatting | bytes 58720256 | tf_op jit(solution)/shard_map/reshape | solution.py:53
  384.2 2.5 broadcast_in_dim.10
  386.8 90.8 %scatter_fusion.2 = f32[64,128,128]{2,1,0:T(8,128)} fusion(f32[64,128,128]{2,1,0:T(8,128)} %broadcast_in_dim.10, s32[448]{0:T(512)S(1)} %bitcast.27, f32[448,128,128]{2,1,0:T(8,128)} %copy.16), kind=kCustom, calls=%fused_computation.4 | custom fusion | flops 7340032 | bytes 88082176 | tf_op jit(solution)/shard_map/scatter-add | solution.py:52
  (15 shorter events, 0.6 us)
Async XLA Ops:
  6.5 20.6 %copy-start = (s32[32,7]{0,1:T(8,128)S(1)}, s32[32,7]{0,1:T(8,128)}, u32[]{:S(2)}) copy-start(s32[32,7]{0,1:T(8,128)} %param.5) | copy-start | bytes 2692
  6.5 84.2 %all-gather.2.cloned.1.call-start = ((), (), s32[]{:S(2)}) async-start(), calls=%async_computation.3 | async-start | bytes 5242880 | tf_op jit(solution)/shard_map/all_gather | solution.py:15
  11.1 11.9 %all-to-all-start = ((bf16[8,8,7]{2,1,0:T(8,128)(2,1)}), bf16[8,8,7]{2,1,0:T(8,128)(2,1)S(1)}, u32[]{:S(2)}, u32[]{:S(2)}) async-start(bf16[8,8,7]{2,1,0:T(8,128)(2,1)} %convert_bitcast_fusion.1), calls=%async_computation | async-start | bytes 32768 | tf_op jit(solution)/shard_map/all_to_all | solution.py:45
  22.9 150.6 %all-to-all-start.2 = ((bf16[64,128,128]{2,1,0:T(8,128)(2,1)}), bf16[64,128,128]{2,1,0:T(8,128)(2,1)S(1)}, u32[]{:S(2)}, u32[]{:S(2)}) async-start(bf16[64,128,128]{2,1,0:T(8,128)(2,1)} %scatter_fusion.1), calls=%async_computation.2 | async-start | bytes 4194304 | tf_op jit(solution)/shard_map/all_to_all | solution.py:43
  173.5 166.5 %all-to-all-start.1 = ((bf16[64,7,128,128]{2,3,1,0:T(8,128)(2,1)}), bf16[64,7,128,128]{2,3,1,0:T(8,128)(2,1)}, u32[]{:S(2)}, u32[]{:S(2)}) async-start(bf16[64,7,128,128]{2,3,1,0:T(8,128)(2,1)} %copy.15), calls=%async_computation.1 | async-start | bytes 29360128 | tf_op jit(solution)/shard_map/all_to_all | solution.py:44
Sparse Core Ops, SparseCore 0:
  8.9 81.8 all-gather.1
where the time goes:
time: 487 us; the launch traced here: 484 us
  waiting for transfers between devices  224 us (46%)
  local copies, waits for them, and re-layouts  113 us (23%)
  other arithmetic  93.8 us (19%)
  matrix products  25.2 us (5%)
  starting transfers between devices  15.2 us (3%)
  between operations  13.4 us (3%)
    all_to_all x1, waiting for transfers between devices, on_device(): lax.all_to_all(factor_buffer, 'wide', split_axis=0, concat_axis=0, tiled=...  160 us
    scatter-add x1, other arithmetic, on_device(): coarse.at[target_index]  90.8 us
    all_gather x1, waiting for transfers between devices, on_device(): gathered = lax.all_gather(p_vals, 'grp', axis=0, tiled=True)  63.4 us
    scatter x2, local copies, waits for them, and re-layouts, on_device(): factor_buffer = jnp.zeros((owners * capacity, per_row, block_side, block_...  42 us
    reshape x1, local copies, waits for them, and re-layouts, on_device(): got_tiles.astype(jnp.float32).reshape(-1, block_side, block_side)  29.5 us
    dot_general x1, matrix products, on_device(): jnp.einsum('rab,rkac->rkbc', got_rows, got_factors, preferred_element_typ...  14.7 us
    convert_element_type x1, local copies, waits for them, and re-layouts, on_device(): products = jnp.einsum('rkab,rkbc->rkac', a_vals, picked, preferred_elemen...  10.7 us
    gather x1, local copies, waits for them, and re-layouts, on_device(): picked = gathered[source_plane * local_rows + offset]  10.6 us
  transfers between devices with their start and end apart: 4, of which 2 were waited for; matrix products, arithmetic and copies ran while one was open for 19% of the time, Pallas kernels for 0%

commit v1 on v0

v1 whole, which is shorter than its diff:
```python
import functools

import jax
import jax.numpy as jnp
from jax import lax
from jax.experimental import pallas as pl
from jax.experimental.pallas import tpu as pltpu
from jax.sharding import PartitionSpec as P

ROW_BLOCK = 4
VMEM_BYTES = 60 * 2**20


def flip(size, bit):
    return [(i, i ^ bit) for i in range(size)]


def transpose_kernel(p_ref, *chunk_refs):
    for row in range(p_ref.shape[0]):
        turned = p_ref[row].T
        first = 0
        for chunk in chunk_refs:
            rows = chunk.shape[1]
            chunk[row] = turned[first : first + rows]
            first += rows


def transposed_chunks(p_vals, heights):
    rows, side, _ = p_vals.shape
    block = 8
    return pl.pallas_call(
        transpose_kernel,
        grid=(rows // block,),
        in_specs=[pl.BlockSpec((block, side, side), lambda i: (i, 0, 0))],
        out_specs=[pl.BlockSpec((block, h, side), lambda i: (i, 0, 0)) for h in heights],
        out_shape=[jax.ShapeDtypeStruct((rows, h, side), p_vals.dtype) for h in heights],
        name="turn",
    )(p_vals)


def partial_kernel(pos_ref, dst_ref, a_ref, p_ref, *refs):
    planes = len(refs) - 4
    parts = refs[:planes]
    send_ref, keep_ref, near, total = refs[planes:]
    step = pl.program_id(0)
    row_block, per_row = a_ref.shape[0], a_ref.shape[1]
    height = near.shape[1]

    @pl.when(step == 0)
    def _():
        rows = parts[0].shape[0]
        for plane, part in enumerate(parts):
            near[plane * rows : (plane + 1) * rows] = part[...]
        total[...] = jnp.zeros_like(total)

    for row in range(row_block):
        entry = (step * row_block + row) * per_row
        products = [
            lax.dot_general(
                near[pos_ref[entry + k]],
                a_ref[row, k],
                (((1,), (1,)), ((), ())),
                preferred_element_type=jnp.float32,
            ).astype(jnp.bfloat16)
            for k in range(per_row)
        ]
        terms = jnp.dot(
            jnp.concatenate(products, axis=0), p_ref[row], preferred_element_type=jnp.float32
        )
        slots = [dst_ref[entry + k] for k in range(per_row)]
        sums = [
            total[slots[k]] + terms[k * height : (k + 1) * height] for k in range(per_row)
        ]
        for k in range(per_row):
            total[slots[k]] = sums[k]

    @pl.when(step == pl.num_programs(0) - 1)
    def _():
        half = keep_ref.shape[0]
        keep_ref[...] = total[:half].astype(keep_ref.dtype)
        send_ref[...] = total[half:].astype(send_ref.dtype)


def partial_sums(pos, dst, a_vals, p_vals, parts, slots):
    rows, per_row, side, _ = a_vals.shape
    height = parts[0].shape[1]
    half = slots // 2
    whole = lambda i, *_: (0, 0, 0)
    return pl.pallas_call(
        partial_kernel,
        grid_spec=pltpu.PrefetchScalarGridSpec(
            num_scalar_prefetch=2,
            grid=(rows // ROW_BLOCK,),
            in_specs=[
                pl.BlockSpec((ROW_BLOCK, per_row, side, side), lambda i, *_: (i, 0, 0, 0)),
                pl.BlockSpec((ROW_BLOCK, side, side), lambda i, *_: (i, 0, 0)),
            ]
            + [pl.BlockSpec((rows, height, side), whole)] * len(parts),
            out_specs=[pl.BlockSpec((half, height, side), whole)] * 2,
            scratch_shapes=[
                pltpu.VMEM((len(parts) * rows, height, side), jnp.bfloat16),
                pltpu.VMEM((slots, height, side), jnp.float32),
            ],
        ),
        out_shape=[jax.ShapeDtypeStruct((half, height, side), jnp.bfloat16)] * 2,
        compiler_params=pltpu.CompilerParams(vmem_limit_bytes=VMEM_BYTES),
        cost_estimate=pl.CostEstimate(
            flops=4 * rows * per_row * height * side * side,
            bytes_accessed=2 * a_vals.size + 2 * p_vals.size + 4 * slots * height * side,
            transcendentals=0,
        ),
        name="partial",
    )(pos, dst, a_vals, p_vals, *parts)


def finish_kernel(*refs):
    *pairs, out_ref = refs
    for slot in range(out_ref.shape[0]):
        sums = [
            pairs[j][slot].astype(jnp.float32) + pairs[j + 1][slot].astype(jnp.float32)
            for j in range(0, len(pairs), 2)
        ]
        out_ref[slot] = jnp.concatenate(sums, axis=0).T


def finish(pairs):
    slots, _, side = pairs[0][0].shape
    block = 8
    flat = [array for pair in pairs for array in pair]
    return pl.pallas_call(
        finish_kernel,
        grid=(slots // block,),
        in_specs=[
            pl.BlockSpec((block, array.shape[1], side), lambda i: (i, 0, 0)) for array in flat
        ],
        out_specs=pl.BlockSpec((block, side, side), lambda i: (i, 0, 0)),
        out_shape=jax.ShapeDtypeStruct((slots, side, side), jnp.float32),
        name="finish",
    )(*flat)


def gather_planes(own, planes):
    got = {0: own}
    if planes == 4:
        got[1] = lax.ppermute(own, "grp", flip(planes, 1))
        got[3] = lax.ppermute(own, "grp", flip(planes, 3))
        got[2] = lax.ppermute(got[3], "grp", flip(planes, 1))
    else:
        for bit in range(1, planes):
            got[bit] = lax.ppermute(own, "grp", flip(planes, bit))
    return [got[plane] for plane in range(planes)]


def halve(array, bits):
    owners = lax.axis_size("wide")
    keep, send = array
    for at, bit in enumerate(bits):
        got = lax.ppermute(send, "wide", flip(owners, bit))
        if at == len(bits) - 1:
            return keep, got
        half = keep.shape[0] // 2
        send = keep[half:] + got[half:]
        keep = keep[:half] + got[:half]


def on_device(slot_count, heights, a_vals, a_cols, p_vals, tile_slot):
    rows = a_vals.shape[0]
    owners, planes = lax.axis_size("wide"), lax.axis_size("grp")
    me, plane = lax.axis_index("wide"), lax.axis_index("grp")
    pos = ((a_cols // (owners * rows)) ^ plane) * rows + a_cols % rows
    relative = (tile_slot // slot_count % owners) ^ me
    bit_count = owners.bit_length() - 1
    orders = [list(range(bit_count))]
    orders.append([0] + orders[0][:0:-1])

    def place(order):
        spot = jnp.zeros_like(relative)
        for bit in order:
            spot = spot * 2 + (relative >> bit) % 2
        return (spot * slot_count + tile_slot % slot_count).reshape(-1)

    places = [place(order) for order in orders]
    pos = pos.reshape(-1)
    chunks = transposed_chunks(p_vals, heights)
    pairs = []
    for j, chunk in enumerate(chunks):
        parts = gather_planes(chunk, planes)
        send, keep = partial_sums(
            pos, places[j % 2], a_vals, p_vals, parts, owners * slot_count
        )
        pairs.append(halve((keep, send), [1 << bit for bit in orders[j % 2]]))
    return finish(pairs)


def solution(mesh):
    owners = mesh.shape["wide"]
    heights = (32, 32, 32, 32)
    placed = (
        P(("grp", "wide"), None, None, None),
        P(("grp", "wide"), None),
        P(("grp", "wide"), None, None),
        P(("grp", "wide"), None),
    )
    return jax.shard_map(
        functools.partial(on_device, 64, heights),
        mesh=mesh,
        in_specs=placed,
        out_specs=P(("grp", "wide"), None, None),
        check_vma=False,
    )
```

time: 487 us -> 220 us (0.45)
  waiting for transfers between devices: 224 us -> 109 us
  local copies, waits for them, and re-layouts: 113 us -> 6.14 us
  other arithmetic: 93.8 us -> 11 us
  Pallas kernels: 0 us -> 66.7 us
  matrix products: 25.2 us -> 0 us
  between operations: 13.4 us -> 0.08 us
  starting transfers between devices: 15.2 us -> 23.8 us
    all_to_all x3 -> x0, waiting for transfers between devices: 160 us -> none  [the longest x1 160 us: on_device(): lax.all_to_all(factor_buffer, 'wide', split_axis=0, concat_axis=0, tiled=...]
    ppermute x0 -> x24, waiting for transfers between devices: none -> 109 us  [the longest x12 60.7 us: halve(): got = lax.ppermute(send, 'wide', flip(owners, bit))]
    scatter-add x1 -> x0, other arithmetic: 90.8 us -> none  [on_device(): coarse.at[target_index]]
    pallas_call x0 -> x6, Pallas kernels: none -> 66.7 us  [the longest x4 56 us: partial_sums(): pl.pallas_call(partial_kernel, grid_spec=pltpu.PrefetchScalarGridSpec(num...]
    all_gather x1 -> x0, waiting for transfers between devices: 63.4 us -> none  [on_device(): gathered = lax.all_gather(p_vals, 'grp', axis=0, tiled=True)]
    scatter x4 -> x0, local copies, waits for them, and re-layouts: 48.2 us -> none  [the longest x2 42 us: on_device(): factor_buffer = jnp.zeros((owners * capacity, per_row, block_side, block_...]
    reshape x1 -> x3, local copies, waits for them, and re-layouts: 29.5 us -> 2 us  [the longest x2 1.35 us: place(): return (spot * slot_count + tile_slot % slot_count).reshape(-1)]
    dot_general x2 -> x0, matrix products: 25.2 us -> none  [the longest x1 14.7 us: on_device(): jnp.einsum('rab,rkac->rkbc', got_rows, got_factors, preferred_element_typ...]
  transfers between devices with their start and end apart: 4 -> 24, of which waited for: 2 -> 14; matrix products, arithmetic and copies ran while one was open for 19% -> 6% of each run, Pallas kernels for 0% -> 26%
where the time goes in v1:
time: 220 us; the launch traced here: 217 us
  waiting for transfers between devices  109 us (50%)
  Pallas kernels  66.7 us (30%)
  starting transfers between devices  23.8 us (11%)
  other arithmetic  11 us (5%)
  local copies, waits for them, and re-layouts  6.14 us (3%)
    ppermute x12, waiting for transfers between devices, halve(): got = lax.ppermute(send, 'wide', flip(owners, bit))  60.7 us
    pallas_call x4, Pallas kernels, partial_sums(): pl.pallas_call(partial_kernel, grid_spec=pltpu.PrefetchScalarGridSpec(num...  56 us
    ppermute x4, waiting for transfers between devices, gather_planes(): got[2] = lax.ppermute(got[3], 'grp', flip(planes, 1))  26.9 us
    ppermute x4, waiting for transfers between devices, gather_planes(): got[1] = lax.ppermute(own, 'grp', flip(planes, 1))  15.8 us
    ppermute x12, starting transfers between devices, halve(): got = lax.ppermute(send, 'wide', flip(owners, bit))  7.52 us
    pallas_call x1, Pallas kernels, finish(): pl.pallas_call(finish_kernel, grid=(slots // block,), in_specs=[pl.BlockS...  7.14 us
    ppermute x4, starting transfers between devices, gather_planes(): got[3] = lax.ppermute(own, 'grp', flip(planes, 3))  6.29 us
    add x4, other arithmetic, halve(): keep = keep[:half] + got[:half]  6 us
  transfers between devices with their start and end apart: 24, of which 14 were waited for; matrix products, arithmetic and copies ran while one was open for 6% of the time, Pallas kernels for 26%

profile of v1, /device:TPU:3, one launch (start us, length us, event | category | flops | bytes accessed | tf_op | source)
XLA Modules:
  0.0 216.9 jit_solution(10179607535754767539)
XLA Ops:
  0.0 3.5 %turn.1 = (bf16[32,32,128]{2,1,0:T(8,128)(2,1)}, bf16[32,32,128]{2,1,0:T(8,128)(2,1)}, bf16[32,32,128]{2,1,0:T(8,128)(2,1)}, bf16[32,32,128]{2,1,0:T(8,128)(2,1)}) custom-call(bf16[32,128,128]{2,1,0:T(8,128)(2,1)} %p_ref.9), custom_call_target="tpu_custom_call" | custom-call | tf_op jit(solution)/shard_map/turn/pallas_call | solution.py:31
  3.5 3.3 %collective-permute-start.19 = (bf16[32,32,128]{2,1,0:T(8,128)(2,1)}, bf16[32,32,128]{2,1,0:T(8,128)(2,1)S(1)}, u32[]{:S(2)}, u32[]{:S(2)}) collective-permute-start(bf16[32,32,128]{2,1,0:T(8,128)(2,1)} %get-tuple-element.26.refs_0_), channel_id=1, source_target_pairs={{0,24},{8,16},{16,8},{24,0},{1,25},{9,17},{17,9},{25,1},{2,26},{10... | collective-permute-start | bytes 786440 | tf_op jit(solution)/shard_map/ppermute | solution.py:146
  7.2 5.8 %collective-permute-done.19.refs_3_ = bf16[32,32,128]{2,1,0:T(8,128)(2,1)S(1)} collective-permute-done((bf16[32,32,128]{2,1,0:T(8,128)(2,1)}, bf16[32,32,128]{2,1,0:T(8,128)(2,1)S(1)}, u32[]{:S(2)}, u32[]{:S(2)}) %collective-permute-start.19) | collective-permute-done | bytes 262176 | tf_op jit(solution)/shard_map/ppermute | solution.py:146
  13.0 5.0 %collective-permute-start.20 = (bf16[32,32,128]{2,1,0:T(8,128)(2,1)S(1)}, bf16[32,32,128]{2,1,0:T(8,128)(2,1)S(1)}, u32[]{:S(2)}, u32[]{:S(2)}) collective-permute-start(bf16[32,32,128]{2,1,0:T(8,128)(2,1)S(1)} %collective-permute-done.19.refs_3_), channel_id=1, source_target_pairs={{0,8},{8,0},{16,24},{24,16},{1,9},{9,1},{17,25},{25,17},{2,10},{10... | collective-permute-start | bytes 786440 | tf_op jit(solution)/shard_map/ppermute | solution.py:147
  21.0 9.8 %collective-permute-done.20.refs_2_ = bf16[32,32,128]{2,1,0:T(8,128)(2,1)S(1)} collective-permute-done((bf16[32,32,128]{2,1,0:T(8,128)(2,1)S(1)}, bf16[32,32,128]{2,1,0:T(8,128)(2,1)S(1)}, u32[]{:S(2)}, u32[]{:S(2)}) %collective-permute-start.20) | collective-permute-done | bytes 262176 | tf_op jit(solution)/shard_map/ppermute | solution.py:147
  31.5 14.0 %partial.7 = (bf16[256,32,128]{2,1,0:T(8,128)(2,1)}, bf16[256,32,128]{2,1,0:T(8,128)(2,1)}) custom-call(s32[224]{0:T(256)} %reshape.9.pos_ref, s32[224]{0:T(256)} %reshape.11.dst_ref, bf16[32,7,128,128]{3,2,1,0:T(8,128)(2,1)} %a_ref.7, bf16[32,128,128]{2,1,0:T(8,128)(2,1)} %p_ref.9, bf16[32,32,128]{2,1,0:T(8,128)(2,1)} %get-tuple-element.26.refs_0_, ...), custom_call_target="tpu_custom_call" | custom-call | flops 469762048 | bytes 16777216 | tf_op jit(solution)/shard_map/partial/pallas_call | solution.py:89
  49.8 3.9 %collective-permute-done.12.refs_1_ = bf16[32,32,128]{2,1,0:T(8,128)(2,1)S(1)} collective-permute-done((bf16[32,32,128]{2,1,0:T(8,128)(2,1)S(1)}, bf16[32,32,128]{2,1,0:T(8,128)(2,1)S(1)}, u32[]{:S(2)}, u32[]{:S(2)}) %collective-permute-start.12) | collective-permute-done | bytes 262176 | tf_op jit(solution)/shard_map/ppermute | solution.py:145
  53.8 5.6 %collective-permute-done.14.refs_2_ = bf16[32,32,128]{2,1,0:T(8,128)(2,1)S(1)} collective-permute-done((bf16[32,32,128]{2,1,0:T(8,128)(2,1)S(1)}, bf16[32,32,128]{2,1,0:T(8,128)(2,1)S(1)}, u32[]{:S(2)}, u32[]{:S(2)}) %collective-permute-start.14) | collective-permute-done | bytes 262176 | tf_op jit(solution)/shard_map/ppermute | solution.py:147
  60.1 14.1 %partial.6 = (bf16[256,32,128]{2,1,0:T(8,128)(2,1)}, bf16[256,32,128]{2,1,0:T(8,128)(2,1)}) custom-call(s32[224]{0:T(256)} %reshape.9.pos_ref, s32[224]{0:T(256)} %reshape.10.dst_ref, bf16[32,7,128,128]{3,2,1,0:T(8,128)(2,1)} %a_ref.7, bf16[32,128,128]{2,1,0:T(8,128)(2,1)} %p_ref.9, bf16[32,32,128]{2,1,0:T(8,128)(2,1)} %get-tuple-element.23.refs_0_, ...), custom_call_target="tpu_custom_call" | custom-call | flops 469762048 | bytes 16777216 | tf_op jit(solution)/shard_map/partial/pallas_call | solution.py:89
  78.2 5.5 %collective-permute-done.6.refs_1_ = bf16[32,32,128]{2,1,0:T(8,128)(2,1)S(1)} collective-permute-done((bf16[32,32,128]{2,1,0:T(8,128)(2,1)S(1)}, bf16[32,32,128]{2,1,0:T(8,128)(2,1)S(1)}, u32[]{:S(2)}, u32[]{:S(2)}) %collective-permute-start.6) | collective-permute-done | bytes 262176 | tf_op jit(solution)/shard_map/ppermute | solution.py:145
  83.7 5.8 %collective-permute-done.8.refs_2_ = bf16[32,32,128]{2,1,0:T(8,128)(2,1)S(1)} collective-permute-done((bf16[32,32,128]{2,1,0:T(8,128)(2,1)S(1)}, bf16[32,32,128]{2,1,0:T(8,128)(2,1)S(1)}, u32[]{:S(2)}, u32[]{:S(2)}) %collective-permute-start.8) | collective-permute-done | bytes 262176 | tf_op jit(solution)/shard_map/ppermute | solution.py:147
  90.3 13.9 %partial.5 = (bf16[256,32,128]{2,1,0:T(8,128)(2,1)}, bf16[256,32,128]{2,1,0:T(8,128)(2,1)}) custom-call(s32[224]{0:T(256)} %reshape.9.pos_ref, s32[224]{0:T(256)} %reshape.11.dst_ref, bf16[32,7,128,128]{3,2,1,0:T(8,128)(2,1)} %a_ref.7, bf16[32,128,128]{2,1,0:T(8,128)(2,1)} %p_ref.9, bf16[32,32,128]{2,1,0:T(8,128)(2,1)} %get-tuple-element.20.refs_0_, ...), custom_call_target="tpu_custom_call" | custom-call | flops 469762048 | bytes 16777216 | tf_op jit(solution)/shard_map/partial/pallas_call | solution.py:89
  106.6 6.3 %collective-permute-done.refs_1_ = bf16[32,32,128]{2,1,0:T(8,128)(2,1)S(1)} collective-permute-done((bf16[32,32,128]{2,1,0:T(8,128)(2,1)S(1)}, bf16[32,32,128]{2,1,0:T(8,128)(2,1)S(1)}, u32[]{:S(2)}, u32[]{:S(2)}) %collective-permute-start) | collective-permute-done | bytes 262176 | tf_op jit(solution)/shard_map/ppermute | solution.py:145
  112.9 5.6 %collective-permute-done.2.refs_2_ = bf16[32,32,128]{2,1,0:T(8,128)(2,1)S(1)} collective-permute-done((bf16[32,32,128]{2,1,0:T(8,128)(2,1)S(1)}, bf16[32,32,128]{2,1,0:T(8,128)(2,1)S(1)}, u32[]{:S(2)}, u32[]{:S(2)}) %collective-permute-start.2) | collective-permute-done | bytes 262176 | tf_op jit(solution)/shard_map/ppermute | solution.py:147
  119.2 14.0 %partial.4 = (bf16[256,32,128]{2,1,0:T(8,128)(2,1)}, bf16[256,32,128]{2,1,0:T(8,128)(2,1)}) custom-call(s32[224]{0:T(256)} %reshape.9.pos_ref, s32[224]{0:T(256)} %reshape.10.dst_ref, bf16[32,7,128,128]{3,2,1,0:T(8,128)(2,1)} %a_ref.7, bf16[32,128,128]{2,1,0:T(8,128)(2,1)} %p_ref.9, bf16[32,32,128]{2,1,0:T(8,128)(2,1)} %get-tuple-element.17.refs_0_, ...), custom_call_target="tpu_custom_call" | custom-call | flops 469762048 | bytes 16777216 | tf_op jit(solution)/shard_map/partial/pallas_call | solution.py:89
  134.2 1.9 slice_add_fusion.1
  137.4 1.9 slice_add_fusion.3
  139.7 1.9 slice_add_fusion.5
  143.4 17.4 %collective-permute-done.22 = bf16[128,32,128]{2,1,0:T(8,128)(2,1)S(1)} collective-permute-done((bf16[128,32,128]{2,1,0:T(8,128)(2,1)S(1)}, bf16[128,32,128]{2,1,0:T(8,128)(2,1)S(1)}, u32[]{:S(2)}, u32[]{:S(2)}) %collective-permute-start.22) | collective-permute-done | bytes 1048608 | tf_op jit(solution)/shard_map/ppermute | solution.py:158
  162.0 1.8 collective-permute-done.16
  165.0 18.3 %collective-permute-done.10 = bf16[128,32,128]{2,1,0:T(8,128)(2,1)S(1)} collective-permute-done((bf16[128,32,128]{2,1,0:T(8,128)(2,1)S(1)}, bf16[128,32,128]{2,1,0:T(8,128)(2,1)S(1)}, u32[]{:S(2)}, u32[]{:S(2)}) %collective-permute-start.10) | collective-permute-done | bytes 1048608 | tf_op jit(solution)/shard_map/ppermute | solution.py:158
  187.5 10.0 %collective-permute-done.23.refs_7_ = bf16[64,32,128]{2,1,0:T(8,128)(2,1)S(1)} collective-permute-done((bf16[64,32,128]{2,1,0:T(8,128)(2,1)S(1)}, bf16[64,32,128]{2,1,0:T(8,128)(2,1)S(1)}, u32[]{:S(2)}, u32[]{:S(2)}) %collective-permute-start.23) | collective-permute-done | bytes 524320 | tf_op jit(solution)/shard_map/ppermute | solution.py:158
  197.5 11.2 %collective-permute-done.11.refs_3_ = bf16[64,32,128]{2,1,0:T(8,128)(2,1)S(1)} collective-permute-done((bf16[64,32,128]{2,1,0:T(8,128)(2,1)S(1)}, bf16[64,32,128]{2,1,0:T(8,128)(2,1)S(1)}, u32[]{:S(2)}, u32[]{:S(2)}) %collective-permute-start.11) | collective-permute-done | bytes 524320 | tf_op jit(solution)/shard_map/ppermute | solution.py:158
  209.7 7.1 %finish.1 = f32[64,128,128]{2,1,0:T(8,128)} custom-call(bf16[64,32,128]{2,1,0:T(8,128)(2,1)} %get-tuple-element.44.refs_0_, bf16[64,32,128]{2,1,0:T(8,128)(2,1)} %copy-done.7, bf16[64,32,128]{2,1,0:T(8,128)(2,1)} %get-tuple-element.42.refs_2_, bf16[64,32,128]{2,1,0:T(8,128)(2,1)} %copy-done.6, bf16[64,32,128]{2,1,0:T(8,128)(2,1)} %get-tuple-element.40.refs_4_, ...), custom_call_target="tpu_custom_call" | custom-call | tf_op jit(solution)/shard_map/finish/pallas_call | solution.py:130
  (92 shorter events, 28.7 us)
Async XLA Ops:
  3.5 9.5 %collective-permute-start.19 = (bf16[32,32,128]{2,1,0:T(8,128)(2,1)}, bf16[32,32,128]{2,1,0:T(8,128)(2,1)S(1)}, u32[]{:S(2)}, u32[]{:S(2)}) collective-permute-start(bf16[32,32,128]{2,1,0:T(8,128)(2,1)} %get-tuple-element.26.refs_0_), channel_id=1, source_target_pairs={{0,24},{8,16},{16,8},{24,0},{1,25},{9,17},{17,9},{25,1},{2,26},{10... | collective-permute-start | bytes 786440 | tf_op jit(solution)/shard_map/ppermute | solution.py:146
  6.8 14.1 %collective-permute-start.18 = (bf16[32,32,128]{2,1,0:T(8,128)(2,1)}, bf16[32,32,128]{2,1,0:T(8,128)(2,1)S(1)}, u32[]{:S(2)}, u32[]{:S(2)}) collective-permute-start(bf16[32,32,128]{2,1,0:T(8,128)(2,1)} %get-tuple-element.26.refs_0_), channel_id=1, source_target_pairs={{0,8},{8,0},{16,24},{24,16},{1,9},{9,1},{17,25},{25,17},{2,10},{10... | collective-permute-start | bytes 786440 | tf_op jit(solution)/shard_map/ppermute | solution.py:145
  6.8 40.6 %collective-permute-start.13 = (bf16[32,32,128]{2,1,0:T(8,128)(2,1)}, bf16[32,32,128]{2,1,0:T(8,128)(2,1)S(1)}, u32[]{:S(2)}, u32[]{:S(2)}) collective-permute-start(bf16[32,32,128]{2,1,0:T(8,128)(2,1)} %get-tuple-element.23.refs_0_), channel_id=1, source_target_pairs={{0,24},{8,16},{16,8},{24,0},{1,25},{9,17},{17,9},{25,1},{2,26},{10... | collective-permute-start | bytes 786440 | tf_op jit(solution)/shard_map/ppermute | solution.py:146
  13.0 17.8 %collective-permute-start.20 = (bf16[32,32,128]{2,1,0:T(8,128)(2,1)S(1)}, bf16[32,32,128]{2,1,0:T(8,128)(2,1)S(1)}, u32[]{:S(2)}, u32[]{:S(2)}) collective-permute-start(bf16[32,32,128]{2,1,0:T(8,128)(2,1)S(1)} %collective-permute-done.19.refs_3_), channel_id=1, source_target_pairs={{0,8},{8,0},{16,24},{24,16},{1,9},{9,1},{17,25},{25,17},{2,10},{10... | collective-permute-start | bytes 786440 | tf_op jit(solution)/shard_map/ppermute | solution.py:147
  45.5 88.7 %collective-permute-start.21 = (bf16[256,32,128]{2,1,0:T(8,128)(2,1)}, bf16[256,32,128]{2,1,0:T(8,128)(2,1)}, u32[]{:S(2)}, u32[]{:S(2)}) collective-permute-start(bf16[256,32,128]{2,1,0:T(8,128)(2,1)} %get-tuple-element.28), channel_id=1, source_target_pairs={{0,1},{1,0},{2,3},{3,2},{4,5},{5,4},{6,7},{7,6},{8,9},{9,8},{10,11... | collective-permute-start | bytes 6291464 | tf_op jit(solution)/shard_map/ppermute | solution.py:158
  46.0 7.8 %collective-permute-start.12 = (bf16[32,32,128]{2,1,0:T(8,128)(2,1)S(1)}, bf16[32,32,128]{2,1,0:T(8,128)(2,1)S(1)}, u32[]{:S(2)}, u32[]{:S(2)}) collective-permute-start(bf16[32,32,128]{2,1,0:T(8,128)(2,1)S(1)} %copy-done.10), channel_id=1, source_target_pairs={{0,8},{8,0},{16,24},{24,16},{1,9},{9,1},{17,25},{25,17},{2,10},{10... | collective-permute-start | bytes 786440 | tf_op jit(solution)/shard_map/ppermute | solution.py:145
  47.4 12.0 %collective-permute-start.14 = (bf16[32,32,128]{2,1,0:T(8,128)(2,1)S(1)}, bf16[32,32,128]{2,1,0:T(8,128)(2,1)S(1)}, u32[]{:S(2)}, u32[]{:S(2)}) collective-permute-start(bf16[32,32,128]{2,1,0:T(8,128)(2,1)S(1)} %collective-permute-done.13.refs_3_), channel_id=1, source_target_pairs={{0,8},{8,0},{16,24},{24,16},{1,9},{9,1},{17,25},{25,17},{2,10},{10... | collective-permute-start | bytes 786440 | tf_op jit(solution)/shard_map/ppermute | solution.py:147
  47.5 29.6 %collective-permute-start.7 = (bf16[32,32,128]{2,1,0:T(8,128)(2,1)S(1)}, bf16[32,32,128]{2,1,0:T(8,128)(2,1)S(1)}, u32[]{:S(2)}, u32[]{:S(2)}) collective-permute-start(bf16[32,32,128]{2,1,0:T(8,128)(2,1)S(1)} %copy-done.9), channel_id=1, source_target_pairs={{0,24},{8,16},{16,8},{24,0},{1,25},{9,17},{17,9},{25,1},{2,26},{10... | collective-permute-start | bytes 786440 | tf_op jit(solution)/shard_map/ppermute | solution.py:146
  74.2 63.2 %collective-permute-start.15 = (bf16[256,32,128]{2,1,0:T(8,128)(2,1)}, bf16[256,32,128]{2,1,0:T(8,128)(2,1)}, u32[]{:S(2)}, u32[]{:S(2)}) collective-permute-start(bf16[256,32,128]{2,1,0:T(8,128)(2,1)} %get-tuple-element.25), channel_id=1, source_target_pairs={{0,1},{1,0},{2,3},{3,2},{4,5},{5,4},{6,7},{7,6},{8,9},{9,8},{10,11... | collective-permute-start | bytes 6291464 | tf_op jit(solution)/shard_map/ppermute | solution.py:158
  75.3 8.5 %collective-permute-start.6 = (bf16[32,32,128]{2,1,0:T(8,128)(2,1)S(1)}, bf16[32,32,128]{2,1,0:T(8,128)(2,1)S(1)}, u32[]{:S(2)}, u32[]{:S(2)}) collective-permute-start(bf16[32,32,128]{2,1,0:T(8,128)(2,1)S(1)} %copy-done.9), channel_id=1, source_target_pairs={{0,8},{8,0},{16,24},{24,16},{1,9},{9,1},{17,25},{25,17},{2,10},{10... | collective-permute-start | bytes 786440 | tf_op jit(solution)/shard_map/ppermute | solution.py:145
  77.1 12.5 %collective-permute-start.8 = (bf16[32,32,128]{2,1,0:T(8,128)(2,1)S(1)}, bf16[32,32,128]{2,1,0:T(8,128)(2,1)S(1)}, u32[]{:S(2)}, u32[]{:S(2)}) collective-permute-start(bf16[32,32,128]{2,1,0:T(8,128)(2,1)S(1)} %collective-permute-done.7.refs_3_), channel_id=1, source_target_pairs={{0,8},{8,0},{16,24},{24,16},{1,9},{9,1},{17,25},{25,17},{2,10},{10... | collective-permute-start | bytes 786440 | tf_op jit(solution)/shard_map/ppermute | solution.py:147
  77.1 29.4 %collective-permute-start.1 = (bf16[32,32,128]{2,1,0:T(8,128)(2,1)S(1)}, bf16[32,32,128]{2,1,0:T(8,128)(2,1)S(1)}, u32[]{:S(2)}, u32[]{:S(2)}) collective-permute-start(bf16[32,32,128]{2,1,0:T(8,128)(2,1)S(1)} %copy-done.8), channel_id=1, source_target_pairs={{0,24},{8,16},{16,8},{24,0},{1,25},{9,17},{17,9},{25,1},{2,26},{10... | collective-permute-start | bytes 786440 | tf_op jit(solution)/shard_map/ppermute | solution.py:146
  104.2 35.4 %collective-permute-start.9 = (bf16[256,32,128]{2,1,0:T(8,128)(2,1)}, bf16[256,32,128]{2,1,0:T(8,128)(2,1)}, u32[]{:S(2)}, u32[]{:S(2)}) collective-permute-start(bf16[256,32,128]{2,1,0:T(8,128)(2,1)} %get-tuple-element.22), channel_id=1, source_target_pairs={{0,1},{1,0},{2,3},{3,2},{4,5},{5,4},{6,7},{7,6},{8,9},{9,8},{10,11... | collective-permute-start | bytes 6291464 | tf_op jit(solution)/shard_map/ppermute | solution.py:158
  105.0 7.9 %collective-permute-start = (bf16[32,32,128]{2,1,0:T(8,128)(2,1)S(1)}, bf16[32,32,128]{2,1,0:T(8,128)(2,1)S(1)}, u32[]{:S(2)}, u32[]{:S(2)}) collective-permute-start(bf16[32,32,128]{2,1,0:T(8,128)(2,1)S(1)} %copy-done.8), channel_id=1, source_target_pairs={{0,8},{8,0},{16,24},{24,16},{1,9},{9,1},{17,25},{25,17},{2,10},{10... | collective-permute-start | bytes 786440 | tf_op jit(solution)/shard_map/ppermute | solution.py:145
  106.5 12.0 %collective-permute-start.2 = (bf16[32,32,128]{2,1,0:T(8,128)(2,1)S(1)}, bf16[32,32,128]{2,1,0:T(8,128)(2,1)S(1)}, u32[]{:S(2)}, u32[]{:S(2)}) collective-permute-start(bf16[32,32,128]{2,1,0:T(8,128)(2,1)S(1)} %collective-permute-done.1.refs_3_), channel_id=1, source_target_pairs={{0,8},{8,0},{16,24},{24,16},{1,9},{9,1},{17,25},{25,17},{2,10},{10... | collective-permute-start | bytes 786440 | tf_op jit(solution)/shard_map/ppermute | solution.py:147
  133.3 8.6 %collective-permute-start.3 = (bf16[256,32,128]{2,1,0:T(8,128)(2,1)}, bf16[256,32,128]{2,1,0:T(8,128)(2,1)S(1)}, u32[]{:S(2)}, u32[]{:S(2)}) collective-permute-start(bf16[256,32,128]{2,1,0:T(8,128)(2,1)} %get-tuple-element.19), channel_id=1, source_target_pairs={{0,1},{1,0},{2,3},{3,2},{4,5},{5,4},{6,7},{7,6},{8,9},{9,8},{10,11... | collective-permute-start | bytes 6291464 | tf_op jit(solution)/shard_map/ppermute | solution.py:158
  136.1 24.8 %collective-permute-start.22 = (bf16[128,32,128]{2,1,0:T(8,128)(2,1)S(1)}, bf16[128,32,128]{2,1,0:T(8,128)(2,1)S(1)}, u32[]{:S(2)}, u32[]{:S(2)}) collective-permute-start(bf16[128,32,128]{2,1,0:T(8,128)(2,1)S(1)} %get-tuple-element.30), channel_id=1, source_target_pairs={{0,4},{1,5},{2,6},{3,7},{4,0},{5,1},{6,2},{7,3},{8,12},{9,13},{10,... | collective-permute-start | bytes 3145736 | tf_op jit(solution)/shard_map/ppermute | solution.py:158
  139.3 24.5 %collective-permute-start.16 = (bf16[128,32,128]{2,1,0:T(8,128)(2,1)S(1)}, bf16[128,32,128]{2,1,0:T(8,128)(2,1)S(1)}, u32[]{:S(2)}, u32[]{:S(2)}) collective-permute-start(bf16[128,32,128]{2,1,0:T(8,128)(2,1)S(1)} %get-tuple-element.32), channel_id=1, source_target_pairs={{0,2},{1,3},{2,0},{3,1},{4,6},{5,7},{6,4},{7,5},{8,10},{9,11},{10,... | collective-permute-start | bytes 3145736 | tf_op jit(solution)/shard_map/ppermute | solution.py:158
  141.6 41.7 %collective-permute-start.10 = (bf16[128,32,128]{2,1,0:T(8,128)(2,1)S(1)}, bf16[128,32,128]{2,1,0:T(8,128)(2,1)S(1)}, u32[]{:S(2)}, u32[]{:S(2)}) collective-permute-start(bf16[128,32,128]{2,1,0:T(8,128)(2,1)S(1)} %get-tuple-element.34), channel_id=1, source_target_pairs={{0,4},{1,5},{2,6},{3,7},{4,0},{5,1},{6,2},{7,3},{8,12},{9,13},{10,... | collective-permute-start | bytes 3145736 | tf_op jit(solution)/shard_map/ppermute | solution.py:158
  142.1 44.2 %collective-permute-start.4 = (bf16[128,32,128]{2,1,0:T(8,128)(2,1)S(1)}, bf16[128,32,128]{2,1,0:T(8,128)(2,1)S(1)}, u32[]{:S(2)}, u32[]{:S(2)}) collective-permute-start(bf16[128,32,128]{2,1,0:T(8,128)(2,1)S(1)} %get-tuple-element.36), channel_id=1, source_target_pairs={{0,2},{1,3},{2,0},{3,1},{4,6},{5,7},{6,4},{7,5},{8,10},{9,11},{10,... | collective-permute-start | bytes 3145736 | tf_op jit(solution)/shard_map/ppermute | solution.py:158
  161.7 35.8 %collective-permute-start.23 = (bf16[64,32,128]{2,1,0:T(8,128)(2,1)S(1)}, bf16[64,32,128]{2,1,0:T(8,128)(2,1)S(1)}, u32[]{:S(2)}, u32[]{:S(2)}) collective-permute-start(bf16[64,32,128]{2,1,0:T(8,128)(2,1)S(1)} %get-tuple-element.37), channel_id=1, source_target_pairs={{0,2},{1,3},{2,0},{3,1},{4,6},{5,7},{6,4},{7,5},{8,10},{9,11},{10,... | collective-permute-start | bytes 1572872 | tf_op jit(solution)/shard_map/ppermute | solution.py:158
  164.7 32.8 %collective-permute-start.17 = (bf16[64,32,128]{2,1,0:T(8,128)(2,1)S(1)}, bf16[64,32,128]{2,1,0:T(8,128)(2,1)S(1)}, u32[]{:S(2)}, u32[]{:S(2)}) collective-permute-start(bf16[64,32,128]{2,1,0:T(8,128)(2,1)S(1)} %get-tuple-element.39), channel_id=1, source_target_pairs={{0,4},{1,5},{2,6},{3,7},{4,0},{5,1},{6,2},{7,3},{8,12},{9,13},{10,... | collective-permute-start | bytes 1572872 | tf_op jit(solution)/shard_map/ppermute | solution.py:158
  184.2 24.6 %collective-permute-start.11 = (bf16[64,32,128]{2,1,0:T(8,128)(2,1)S(1)}, bf16[64,32,128]{2,1,0:T(8,128)(2,1)S(1)}, u32[]{:S(2)}, u32[]{:S(2)}) collective-permute-start(bf16[64,32,128]{2,1,0:T(8,128)(2,1)S(1)} %get-tuple-element.41), channel_id=1, source_target_pairs={{0,2},{1,3},{2,0},{3,1},{4,6},{5,7},{6,4},{7,5},{8,10},{9,11},{10,... | collective-permute-start | bytes 1572872 | tf_op jit(solution)/shard_map/ppermute | solution.py:158
  187.2 21.6 %collective-permute-start.5 = (bf16[64,32,128]{2,1,0:T(8,128)(2,1)S(1)}, bf16[64,32,128]{2,1,0:T(8,128)(2,1)S(1)}, u32[]{:S(2)}, u32[]{:S(2)}) collective-permute-start(bf16[64,32,128]{2,1,0:T(8,128)(2,1)S(1)} %get-tuple-element.43), channel_id=1, source_target_pairs={{0,4},{1,5},{2,6},{3,7},{4,0},{5,1},{6,2},{7,3},{8,12},{9,13},{10,... | collective-permute-start | bytes 1572872 | tf_op jit(solution)/shard_map/ppermute | solution.py:158
  (23 other events, 224.9 us)

commit v2 on v0

v2 whole, which is shorter than its diff:
```python
import jax
import jax.numpy as jnp
from jax import lax
from jax.experimental import pallas as pl
from jax.experimental.pallas import tpu as pltpu
from jax.sharding import PartitionSpec as P

SLOT_DEV = 64
MIB = 2**20
VMEM = pl.BlockSpec(memory_space=pltpu.VMEM)
SMEM = pl.BlockSpec(memory_space=pltpu.SMEM)


def flip(size, bit):
    return [(i, i ^ bit) for i in range(size)]


def unit(side):
    shape = (side, side)
    same = lax.broadcasted_iota(jnp.int32, shape, 0) == lax.broadcasted_iota(jnp.int32, shape, 1)
    return same.astype(jnp.bfloat16)


def across(left, right, axes):
    return lax.dot_general(
        left, right, (((axes[0],), (axes[1],)), ((), ())), preferred_element_type=jnp.float32
    )


def turn_kernel(p_ref, *chunk_refs):
    eye = unit(p_ref.shape[1])
    for row in range(p_ref.shape[0]):
        turned = across(eye, p_ref[row], (1, 1)).astype(jnp.bfloat16)
        first = 0
        for chunk in chunk_refs:
            chunk[row] = turned[first : first + chunk.shape[1]]
            first += chunk.shape[1]


def turned_chunks(p_vals, heights):
    rows, side, _ = p_vals.shape
    block = rows // 2
    return pl.pallas_call(
        turn_kernel,
        grid=(rows // block,),
        in_specs=[pl.BlockSpec((block, side, side), lambda i: (i, 0, 0))],
        out_specs=[pl.BlockSpec((block, h, side), lambda i: (i, 0, 0)) for h in heights],
        out_shape=[jax.ShapeDtypeStruct((rows, h, side), p_vals.dtype) for h in heights],
        compiler_params=pltpu.CompilerParams(vmem_limit_bytes=8 * MIB),
        name="turn",
    )(p_vals)


def factor_kernel(a_ref, p_ref, factor_ref):
    block, per_row = a_ref.shape[0], a_ref.shape[1]
    first = pl.program_id(0) * block
    for row in range(block):
        for k in range(per_row):
            factor_ref[first + row, k] = across(a_ref[row, k], p_ref[row], (0, 0)).astype(
                jnp.bfloat16
            )


def factors(a_vals, p_vals):
    rows, per_row, side, _ = a_vals.shape
    block = 8
    return pl.pallas_call(
        factor_kernel,
        grid=(rows // block,),
        in_specs=[
            pl.BlockSpec((block, per_row, side, side), lambda i: (i, 0, 0, 0)),
            pl.BlockSpec((block, side, side), lambda i: (i, 0, 0)),
        ],
        out_specs=VMEM,
        out_shape=jax.ShapeDtypeStruct(a_vals.shape, jnp.bfloat16),
        compiler_params=pltpu.CompilerParams(vmem_limit_bytes=20 * MIB),
        cost_estimate=pl.CostEstimate(
            flops=2 * a_vals.size * side, bytes_accessed=4 * a_vals.size, transcendentals=0
        ),
        name="factors",
    )(a_vals, p_vals)


def partial_kernel(pos_ref, dst_ref, factor_ref, *refs):
    planes = len(refs) - 4
    parts = refs[:planes]
    send_ref, keep_ref, near, total = refs[planes:]
    rows, per_row = factor_ref.shape[0], factor_ref.shape[1]
    block = 8
    total[...] = jnp.zeros_like(total)
    for plane, part in enumerate(parts):
        near[plane * rows : (plane + 1) * rows] = part[...]

    def some_rows(step, carry):
        for at in range(block):
            row = step * block + at
            terms = [
                jnp.dot(
                    near[pos_ref[k, row]],
                    factor_ref[row, k],
                    preferred_element_type=jnp.float32,
                )
                for k in range(per_row)
            ]
            slots = [dst_ref[k, row] for k in range(per_row)]
            sums = [total[slots[k]] + terms[k] for k in range(per_row)]
            for k in range(per_row):
                total[slots[k]] = sums[k]
        return carry

    lax.fori_loop(0, rows // block, some_rows, 0)
    half = keep_ref.shape[0]
    send_ref[...] = total[half:].astype(send_ref.dtype)
    keep_ref[...] = total[:half].astype(keep_ref.dtype)


def partial_sums(pos, dst, factor, parts, slots):
    rows, per_row, side, _ = factor.shape
    height = parts[0].shape[1]
    half = slots // 2
    return pl.pallas_call(
        partial_kernel,
        in_specs=[SMEM, SMEM, VMEM] + [VMEM] * len(parts),
        out_specs=[VMEM, VMEM],
        out_shape=[jax.ShapeDtypeStruct((half, height, side), jnp.bfloat16)] * 2,
        scratch_shapes=[
            pltpu.VMEM((len(parts) * rows, height, side), jnp.bfloat16),
            pltpu.VMEM((slots, height, side), jnp.float32),
        ],
        compiler_params=pltpu.CompilerParams(
            vmem_limit_bytes=4 * slots * height * side + 3 * MIB
        ),
        cost_estimate=pl.CostEstimate(
            flops=2 * rows * per_row * height * side * side,
            bytes_accessed=2 * factor.size + 2 * slots * height * side,
            transcendentals=0,
        ),
        name="partial",
    )(pos, dst, factor, *parts)


def finish_kernel(*refs):
    *pairs, out_ref = refs
    eye = unit(out_ref.shape[1])
    twice = jnp.concatenate([eye, eye], axis=1)
    for slot in range(out_ref.shape[0]):
        kept = jnp.concatenate([ref[slot] for ref in pairs[0::2]], axis=0)
        got = jnp.concatenate([ref[slot] for ref in pairs[1::2]], axis=0)
        out_ref[slot] = across(twice, jnp.concatenate([kept, got], axis=1), (1, 1))


def finish(pairs):
    slots, _, side = pairs[0][0].shape
    block = slots // 2
    flat = [array for pair in pairs for array in pair]
    return pl.pallas_call(
        finish_kernel,
        grid=(slots // block,),
        in_specs=[
            pl.BlockSpec((block, array.shape[1], side), lambda i: (i, 0, 0)) for array in flat
        ],
        out_specs=pl.BlockSpec((block, side, side), lambda i: (i, 0, 0)),
        out_shape=jax.ShapeDtypeStruct((slots, side, side), jnp.float32),
        compiler_params=pltpu.CompilerParams(vmem_limit_bytes=16 * MIB),
        name="finish",
    )(*flat)


def on_device(heights, orders, a_vals, a_cols, p_vals, tile_slot):
    rows = a_vals.shape[0]
    owners, planes = lax.axis_size("wide"), lax.axis_size("grp")
    me, plane = lax.axis_index("wide"), lax.axis_index("grp")
    columns, slots = a_cols.T, tile_slot.T
    pos = ((columns // (owners * rows)) ^ plane) * rows + columns % rows
    relative = (slots // SLOT_DEV % owners) ^ me
    places = []
    for order in orders:
        spot = jnp.zeros_like(relative)
        for bit in order:
            spot = spot * 2 + (relative >> bit) % 2
        places.append(spot * SLOT_DEV + slots % SLOT_DEV)
    chunks = turned_chunks(p_vals, heights)
    factor = factors(a_vals, p_vals)
    pairs = []
    for j, own in enumerate(chunks):
        got = {0: own}
        for bit in reversed(range(1, planes)):
            relay = planes == 4 and bit == 2
            got[bit] = lax.ppermute(
                got[3] if relay else own, "grp", flip(planes, 1 if relay else bit)
            )
        order = orders[j % len(orders)]
        send, keep = partial_sums(
            pos,
            places[j % len(orders)],
            factor,
            [got[bit] for bit in range(planes)],
            owners * SLOT_DEV,
        )
        for at, bit in enumerate(order):
            back = lax.ppermute(send, "wide", flip(owners, 1 << bit))
            if at == len(order) - 1:
                pairs.append((keep, back))
                break
            half = keep.shape[0] // 2
            send, keep = keep[half:] + back[half:], keep[:half] + back[:half]
    return finish(pairs)


def solution(mesh):
    owners = mesh.shape["wide"]
    moves = owners.bit_length() - 1
    height = max(16, min(32, 32 * 8 // owners))
    heights = (height,) * (128 // height)
    orders = [list(range(moves))]
    orders.append([0] + orders[0][:0:-1])
    placed = (
        P(("grp", "wide"), None, None, None),
        P(("grp", "wide"), None),
        P(("grp", "wide"), None, None),
        P(("grp", "wide"), None),
    )

    def program(*arrays):
        return on_device(heights, orders, *arrays)

    return jax.shard_map(
        program,
        mesh=mesh,
        in_specs=placed,
        out_specs=P(("grp", "wide"), None, None),
        check_vma=False,
    )
```

time: 487 us -> 170 us (0.35)
  waiting for transfers between devices: 224 us -> 107 us
  local copies, waits for them, and re-layouts: 113 us -> 11.5 us
  other arithmetic: 93.8 us -> 1.31 us
  matrix products: 25.2 us -> 0 us
  Pallas kernels: 0 us -> 22.8 us
  between operations: 13.4 us -> 0.13 us
  starting transfers between devices: 15.2 us -> 24.8 us
    all_to_all x3 -> x0, waiting for transfers between devices: 160 us -> none  [the longest x1 160 us: on_device(): lax.all_to_all(factor_buffer, 'wide', split_axis=0, concat_axis=0, tiled=...]
    ppermute x0 -> x24, waiting for transfers between devices: none -> 107 us  [the longest x12 65.9 us: on_device(): back = lax.ppermute(send, 'wide', flip(owners, 1 << bit))]
    scatter-add x1 -> x0, other arithmetic: 90.8 us -> none  [on_device(): coarse.at[target_index]]
    all_gather x1 -> x0, waiting for transfers between devices: 63.4 us -> none  [on_device(): gathered = lax.all_gather(p_vals, 'grp', axis=0, tiled=True)]
    scatter x4 -> x0, local copies, waits for them, and re-layouts: 48.2 us -> none  [the longest x2 42 us: on_device(): factor_buffer = jnp.zeros((owners * capacity, per_row, block_side, block_...]
    reshape x1 -> x0, local copies, waits for them, and re-layouts: 29.5 us -> none  [on_device(): got_tiles.astype(jnp.float32).reshape(-1, block_side, block_side)]
    dot_general x2 -> x0, matrix products: 25.2 us -> none  [the longest x1 14.7 us: on_device(): jnp.einsum('rab,rkac->rkbc', got_rows, got_factors, preferred_element_typ...]
    ppermute x0 -> x24, starting transfers between devices: none -> 24.8 us  [the longest x12 16.9 us: on_device(): lax.ppermute(got[3] if relay else own, 'grp', flip(planes, 1 if relay els...]
  transfers between devices with their start and end apart: 4 -> 24, of which waited for: 2 -> 15; matrix products, arithmetic and copies ran while one was open for 19% -> 1% of each run, Pallas kernels for 0% -> 11%
where the time goes in v2:
time: 170 us; the launch traced here: 167 us
  waiting for transfers between devices  107 us (63%)
  starting transfers between devices  24.8 us (15%)
  Pallas kernels  22.8 us (13%)
  local copies, waits for them, and re-layouts  11.5 us (7%)
    ppermute x12, waiting for transfers between devices, on_device(): back = lax.ppermute(send, 'wide', flip(owners, 1 << bit))  65.9 us
    ppermute x12, waiting for transfers between devices, on_device(): lax.ppermute(got[3] if relay else own, 'grp', flip(planes, 1 if relay els...  41 us
    ppermute x12, starting transfers between devices, on_device(): lax.ppermute(got[3] if relay else own, 'grp', flip(planes, 1 if relay els...  16.9 us
    pallas_call x4, Pallas kernels, partial_sums(): pl.pallas_call(partial_kernel, in_specs=[SMEM, SMEM, VMEM] + [VMEM] * len...  16.3 us
    unnamed x14, local copies, waits for them, and re-layouts  11.5 us
    ppermute x12, starting transfers between devices, on_device(): back = lax.ppermute(send, 'wide', flip(owners, 1 << bit))  7.94 us
  transfers between devices with their start and end apart: 24, of which 15 were waited for; matrix products, arithmetic and copies ran while one was open for 1% of the time, Pallas kernels for 11%

profile of v2, /device:TPU:3, one launch (start us, length us, event | category | flops | bytes accessed | tf_op | source)
XLA Modules:
  0.0 167.5 jit_solution(7614586298145779570)
XLA Ops:
  2.2 3.4 %collective-permute-start.19 = (bf16[32,32,128]{2,1,0:T(8,128)(2,1)S(1)}, bf16[32,32,128]{2,1,0:T(8,128)(2,1)S(1)}, u32[]{:S(2)}, u32[]{:S(2)}) collective-permute-start(bf16[32,32,128]{2,1,0:T(8,128)(2,1)S(1)} %get-tuple-element.26.refs_0_), channel_id=1, source_target_pairs={{0,24},{8,16},{16,8},{24,0},{1,25},{9,17},{17,9},{25,1},{2,26},{10... | collective-permute-start | bytes 786440 | tf_op jit(solution)/shard_map/ppermute | solution.py:189
  5.9 5.6 %collective-permute-done.19.refs_3_ = bf16[32,32,128]{2,1,0:T(8,128)(2,1)S(1)} collective-permute-done((bf16[32,32,128]{2,1,0:T(8,128)(2,1)S(1)}, bf16[32,32,128]{2,1,0:T(8,128)(2,1)S(1)}, u32[]{:S(2)}, u32[]{:S(2)}) %collective-permute-start.19) | collective-permute-done | bytes 262176 | tf_op jit(solution)/shard_map/ppermute | solution.py:189
  11.5 5.0 %collective-permute-start.20 = (bf16[32,32,128]{2,1,0:T(8,128)(2,1)S(1)}, bf16[32,32,128]{2,1,0:T(8,128)(2,1)S(1)}, u32[]{:S(2)}, u32[]{:S(2)}) collective-permute-start(bf16[32,32,128]{2,1,0:T(8,128)(2,1)S(1)} %collective-permute-done.19.refs_3_), channel_id=1, source_target_pairs={{0,8},{8,0},{16,24},{24,16},{1,9},{9,1},{17,25},{25,17},{2,10},{10... | collective-permute-start | bytes 786440 | tf_op jit(solution)/shard_map/ppermute | solution.py:189
  16.6 3.1 %copy-done.2 = bf16[32,7,128,128]{3,2,1,0:T(8,128)(2,1)S(1)} copy-done((bf16[32,7,128,128]{3,2,1,0:T(8,128)(2,1)S(1)}, bf16[32,7,128,128]{3,2,1,0:T(8,128)(2,1)}, u32[]{:S(2)}) %copy-start.2) | copy-done | bytes 7340056
  20.9 2.8 %factors.1.factor_ref = bf16[32,7,128,128]{3,2,1,0:T(8,128)(2,1)S(1)} custom-call(bf16[32,7,128,128]{3,2,1,0:T(8,128)(2,1)S(1)} %copy-done.2, bf16[32,128,128]{2,1,0:T(8,128)(2,1)S(1)} %copy-done.4), custom_call_target="tpu_custom_call" | custom-call | flops 939524096 | bytes 14680064 | tf_op jit(solution)/shard_map/factors/pallas_call | solution.py:67
  23.7 2.9 %copy-done = bf16[32,7,128,128]{3,2,1,0:T(8,128)(2,1)} copy-done((bf16[32,7,128,128]{3,2,1,0:T(8,128)(2,1)}, bf16[32,7,128,128]{3,2,1,0:T(8,128)(2,1)S(1)}, u32[]{:S(2)}) %copy-start) | copy-done | bytes 7340056
  26.6 2.7 %collective-permute-done.20.refs_2_ = bf16[32,32,128]{2,1,0:T(8,128)(2,1)S(1)} collective-permute-done((bf16[32,32,128]{2,1,0:T(8,128)(2,1)S(1)}, bf16[32,32,128]{2,1,0:T(8,128)(2,1)S(1)}, u32[]{:S(2)}, u32[]{:S(2)}) %collective-permute-start.20) | collective-permute-done | bytes 262176 | tf_op jit(solution)/shard_map/ppermute | solution.py:189
  29.3 3.1 %copy-done.1 = bf16[32,7,128,128]{3,2,1,0:T(8,128)(2,1)S(1)} copy-done((bf16[32,7,128,128]{3,2,1,0:T(8,128)(2,1)S(1)}, bf16[32,7,128,128]{3,2,1,0:T(8,128)(2,1)}, u32[]{:S(2)}) %copy-start.1) | copy-done | bytes 7340056
  32.4 4.1 %partial.7 = (bf16[256,32,128]{2,1,0:T(8,128)(2,1)S(1)}, bf16[256,32,128]{2,1,0:T(8,128)(2,1)S(1)}) custom-call(s32[7,32]{1,0:T(8,128)S(1)} %get-tuple-element.47.pos_ref, s32[7,32]{1,0:T(8,128)S(1)} %get-tuple-element.45.dst_ref, bf16[32,7,128,128]{3,2,1,0:T(8,128)(2,1)S(1)} %copy-done.1, bf16[32,32,128]{2,1,0:T(8,128)(2,1)S(1)} %get-tuple-element.26.refs_0_, ...), custom_call_target="tpu_custom_call" | custom-call | flops 234881024 | bytes 11534336 | tf_op jit(solution)/shard_map/partial/pallas_call | solution.py:121
  40.5 4.7 %collective-permute-done.12.refs_1_ = bf16[32,32,128]{2,1,0:T(8,128)(2,1)S(1)} collective-permute-done((bf16[32,32,128]{2,1,0:T(8,128)(2,1)S(1)}, bf16[32,32,128]{2,1,0:T(8,128)(2,1)S(1)}, u32[]{:S(2)}, u32[]{:S(2)}) %collective-permute-start.12) | collective-permute-done | bytes 262176 | tf_op jit(solution)/shard_map/ppermute | solution.py:189
  45.2 5.6 %collective-permute-done.14.refs_2_ = bf16[32,32,128]{2,1,0:T(8,128)(2,1)S(1)} collective-permute-done((bf16[32,32,128]{2,1,0:T(8,128)(2,1)S(1)}, bf16[32,32,128]{2,1,0:T(8,128)(2,1)S(1)}, u32[]{:S(2)}, u32[]{:S(2)}) %collective-permute-start.14) | collective-permute-done | bytes 262176 | tf_op jit(solution)/shard_map/ppermute | solution.py:189
  50.9 4.1 %partial.6 = (bf16[256,32,128]{2,1,0:T(8,128)(2,1)S(1)}, bf16[256,32,128]{2,1,0:T(8,128)(2,1)S(1)}) custom-call(s32[7,32]{1,0:T(8,128)S(1)} %get-tuple-element.47.pos_ref, s32[7,32]{1,0:T(8,128)S(1)} %get-tuple-element.46.dst_ref, bf16[32,7,128,128]{3,2,1,0:T(8,128)(2,1)S(1)} %copy-done.1, bf16[32,32,128]{2,1,0:T(8,128)(2,1)S(1)} %get-tuple-element.23.refs_0_, ...), custom_call_target="tpu_custom_call" | custom-call | flops 234881024 | bytes 11534336 | tf_op jit(solution)/shard_map/partial/pallas_call | solution.py:121
  57.5 1.8 %collective-permute-start.1 = (bf16[32,32,128]{2,1,0:T(8,128)(2,1)S(1)}, bf16[32,32,128]{2,1,0:T(8,128)(2,1)S(1)}, u32[]{:S(2)}, u32[]{:S(2)}) collective-permute-start(bf16[32,32,128]{2,1,0:T(8,128)(2,1)S(1)} %get-tuple-element.17.refs_0_), channel_id=1, source_target_pairs={{0,24},{8,16},{16,8},{24,0},{1,25},{9,17},{17,9},{25,1},{2,26},{10... | collective-permute-start | bytes 786440 | tf_op jit(solution)/shard_map/ppermute | solution.py:189
  59.3 4.5 %collective-permute-done.6.refs_1_ = bf16[32,32,128]{2,1,0:T(8,128)(2,1)S(1)} collective-permute-done((bf16[32,32,128]{2,1,0:T(8,128)(2,1)S(1)}, bf16[32,32,128]{2,1,0:T(8,128)(2,1)S(1)}, u32[]{:S(2)}, u32[]{:S(2)}) %collective-permute-start.6) | collective-permute-done | bytes 262176 | tf_op jit(solution)/shard_map/ppermute | solution.py:189
  63.9 5.6 %collective-permute-done.8.refs_2_ = bf16[32,32,128]{2,1,0:T(8,128)(2,1)S(1)} collective-permute-done((bf16[32,32,128]{2,1,0:T(8,128)(2,1)S(1)}, bf16[32,32,128]{2,1,0:T(8,128)(2,1)S(1)}, u32[]{:S(2)}, u32[]{:S(2)}) %collective-permute-start.8) | collective-permute-done | bytes 262176 | tf_op jit(solution)/shard_map/ppermute | solution.py:189
  69.5 4.1 %partial.5 = (bf16[256,32,128]{2,1,0:T(8,128)(2,1)S(1)}, bf16[256,32,128]{2,1,0:T(8,128)(2,1)S(1)}) custom-call(s32[7,32]{1,0:T(8,128)S(1)} %get-tuple-element.47.pos_ref, s32[7,32]{1,0:T(8,128)S(1)} %get-tuple-element.45.dst_ref, bf16[32,7,128,128]{3,2,1,0:T(8,128)(2,1)S(1)} %copy-done.1, bf16[32,32,128]{2,1,0:T(8,128)(2,1)S(1)} %get-tuple-element.20.refs_0_, ...), custom_call_target="tpu_custom_call" | custom-call | flops 234881024 | bytes 11534336 | tf_op jit(solution)/shard_map/partial/pallas_call | solution.py:121
  76.6 6.6 %collective-permute-done.refs_1_ = bf16[32,32,128]{2,1,0:T(8,128)(2,1)S(1)} collective-permute-done((bf16[32,32,128]{2,1,0:T(8,128)(2,1)S(1)}, bf16[32,32,128]{2,1,0:T(8,128)(2,1)S(1)}, u32[]{:S(2)}, u32[]{:S(2)}) %collective-permute-start) | collective-permute-done | bytes 262176 | tf_op jit(solution)/shard_map/ppermute | solution.py:189
  83.1 5.6 %collective-permute-done.2.refs_2_ = bf16[32,32,128]{2,1,0:T(8,128)(2,1)S(1)} collective-permute-done((bf16[32,32,128]{2,1,0:T(8,128)(2,1)S(1)}, bf16[32,32,128]{2,1,0:T(8,128)(2,1)S(1)}, u32[]{:S(2)}, u32[]{:S(2)}) %collective-permute-start.2) | collective-permute-done | bytes 262176 | tf_op jit(solution)/shard_map/ppermute | solution.py:189
  88.8 4.1 %partial.4 = (bf16[256,32,128]{2,1,0:T(8,128)(2,1)S(1)}, bf16[256,32,128]{2,1,0:T(8,128)(2,1)S(1)}) custom-call(s32[7,32]{1,0:T(8,128)S(1)} %get-tuple-element.47.pos_ref, s32[7,32]{1,0:T(8,128)S(1)} %get-tuple-element.46.dst_ref, bf16[32,7,128,128]{3,2,1,0:T(8,128)(2,1)S(1)} %copy-done.1, bf16[32,32,128]{2,1,0:T(8,128)(2,1)S(1)} %get-tuple-element.17.refs_0_, ...), custom_call_target="tpu_custom_call" | custom-call | flops 234881024 | bytes 11534336 | tf_op jit(solution)/shard_map/partial/pallas_call | solution.py:121
  97.9 20.6 %collective-permute-done.22 = bf16[128,32,128]{2,1,0:T(8,128)(2,1)S(1)} collective-permute-done((bf16[128,32,128]{2,1,0:T(8,128)(2,1)S(1)}, bf16[128,32,128]{2,1,0:T(8,128)(2,1)S(1)}, u32[]{:S(2)}, u32[]{:S(2)}) %collective-permute-start.22) | collective-permute-done | bytes 1048608 | tf_op jit(solution)/shard_map/ppermute | solution.py:201
  120.4 20.6 %collective-permute-done.10 = bf16[128,32,128]{2,1,0:T(8,128)(2,1)S(1)} collective-permute-done((bf16[128,32,128]{2,1,0:T(8,128)(2,1)S(1)}, bf16[128,32,128]{2,1,0:T(8,128)(2,1)S(1)}, u32[]{:S(2)}, u32[]{:S(2)}) %collective-permute-start.10) | collective-permute-done | bytes 1048608 | tf_op jit(solution)/shard_map/ppermute | solution.py:201
  142.9 10.6 %collective-permute-done.23.refs_7_ = bf16[64,32,128]{2,1,0:T(8,128)(2,1)S(1)} collective-permute-done((bf16[64,32,128]{2,1,0:T(8,128)(2,1)S(1)}, bf16[64,32,128]{2,1,0:T(8,128)(2,1)S(1)}, u32[]{:S(2)}, u32[]{:S(2)}) %collective-permute-start.23) | collective-permute-done | bytes 524320 | tf_op jit(solution)/shard_map/ppermute | solution.py:201
  153.5 11.2 %collective-permute-done.11.refs_3_ = bf16[64,32,128]{2,1,0:T(8,128)(2,1)S(1)} collective-permute-done((bf16[64,32,128]{2,1,0:T(8,128)(2,1)S(1)}, bf16[64,32,128]{2,1,0:T(8,128)(2,1)S(1)}, u32[]{:S(2)}, u32[]{:S(2)}) %collective-permute-start.11) | collective-permute-done | bytes 524320 | tf_op jit(solution)/shard_map/ppermute | solution.py:201
  164.7 2.8 %finish.1 = f32[64,128,128]{2,1,0:T(8,128)} custom-call(bf16[64,32,128]{2,1,0:T(8,128)(2,1)S(1)} %get-tuple-element.44.refs_0_, bf16[64,32,128]{2,1,0:T(8,128)(2,1)S(1)} %collective-permute-done.5.refs_1_, bf16[64,32,128]{2,1,0:T(8,128)(2,1)S(1)} %get-tuple-element.42.refs_2_, bf16[64,32,128]{2,1,0:T(8,128)(2,1)S(1)} %collective-permute-done.11.refs_3_, ...), custom_call_target="tpu_custom_call" | custom-call | tf_op jit(solution)/shard_map/finish/pallas_call | solution.py:156
  (54 shorter events, 22.2 us)
Async XLA Ops:
  2.2 9.3 %collective-permute-start.19 = (bf16[32,32,128]{2,1,0:T(8,128)(2,1)S(1)}, bf16[32,32,128]{2,1,0:T(8,128)(2,1)S(1)}, u32[]{:S(2)}, u32[]{:S(2)}) collective-permute-start(bf16[32,32,128]{2,1,0:T(8,128)(2,1)S(1)} %get-tuple-element.26.refs_0_), channel_id=1, source_target_pairs={{0,24},{8,16},{16,8},{24,0},{1,25},{9,17},{17,9},{25,1},{2,26},{10... | collective-permute-start | bytes 786440 | tf_op jit(solution)/shard_map/ppermute | solution.py:189
  5.6 21.0 %collective-permute-start.18 = (bf16[32,32,128]{2,1,0:T(8,128)(2,1)S(1)}, bf16[32,32,128]{2,1,0:T(8,128)(2,1)S(1)}, u32[]{:S(2)}, u32[]{:S(2)}) collective-permute-start(bf16[32,32,128]{2,1,0:T(8,128)(2,1)S(1)} %get-tuple-element.26.refs_0_), channel_id=1, source_target_pairs={{0,8},{8,0},{16,24},{24,16},{1,9},{9,1},{17,25},{25,17},{2,10},{10... | collective-permute-start | bytes 786440 | tf_op jit(solution)/shard_map/ppermute | solution.py:189
  5.6 32.9 %collective-permute-start.13 = (bf16[32,32,128]{2,1,0:T(8,128)(2,1)S(1)}, bf16[32,32,128]{2,1,0:T(8,128)(2,1)S(1)}, u32[]{:S(2)}, u32[]{:S(2)}) collective-permute-start(bf16[32,32,128]{2,1,0:T(8,128)(2,1)S(1)} %get-tuple-element.23.refs_0_), channel_id=1, source_target_pairs={{0,24},{8,16},{16,8},{24,0},{1,25},{9,17},{17,9},{25,1},{2,26},{10... | collective-permute-start | bytes 786440 | tf_op jit(solution)/shard_map/ppermute | solution.py:189
  11.5 17.8 %collective-permute-start.20 = (bf16[32,32,128]{2,1,0:T(8,128)(2,1)S(1)}, bf16[32,32,128]{2,1,0:T(8,128)(2,1)S(1)}, u32[]{:S(2)}, u32[]{:S(2)}) collective-permute-start(bf16[32,32,128]{2,1,0:T(8,128)(2,1)S(1)} %collective-permute-done.19.refs_3_), channel_id=1, source_target_pairs={{0,8},{8,0},{16,24},{24,16},{1,9},{9,1},{17,25},{25,17},{2,10},{10... | collective-permute-start | bytes 786440 | tf_op jit(solution)/shard_map/ppermute | solution.py:189
  36.5 57.1 %collective-permute-start.21 = (bf16[256,32,128]{2,1,0:T(8,128)(2,1)S(1)}, bf16[256,32,128]{2,1,0:T(8,128)(2,1)S(1)}, u32[]{:S(2)}, u32[]{:S(2)}) collective-permute-start(bf16[256,32,128]{2,1,0:T(8,128)(2,1)S(1)} %get-tuple-element.28), channel_id=1, source_target_pairs={{0,1},{1,0},{2,3},{3,2},{4,5},{5,4},{6,7},{7,6},{8,9},{9,8},{10,11... | collective-permute-start | bytes 6291464 | tf_op jit(solution)/shard_map/ppermute | solution.py:201
  37.5 7.8 %collective-permute-start.12 = (bf16[32,32,128]{2,1,0:T(8,128)(2,1)S(1)}, bf16[32,32,128]{2,1,0:T(8,128)(2,1)S(1)}, u32[]{:S(2)}, u32[]{:S(2)}) collective-permute-start(bf16[32,32,128]{2,1,0:T(8,128)(2,1)S(1)} %get-tuple-element.23.refs_0_), channel_id=1, source_target_pairs={{0,8},{8,0},{16,24},{24,16},{1,9},{9,1},{17,25},{25,17},{2,10},{10... | collective-permute-start | bytes 786440 | tf_op jit(solution)/shard_map/ppermute | solution.py:189
  38.5 12.4 %collective-permute-start.14 = (bf16[32,32,128]{2,1,0:T(8,128)(2,1)S(1)}, bf16[32,32,128]{2,1,0:T(8,128)(2,1)S(1)}, u32[]{:S(2)}, u32[]{:S(2)}) collective-permute-start(bf16[32,32,128]{2,1,0:T(8,128)(2,1)S(1)} %collective-permute-done.13.refs_3_), channel_id=1, source_target_pairs={{0,8},{8,0},{16,24},{24,16},{1,9},{9,1},{17,25},{25,17},{2,10},{10... | collective-permute-start | bytes 786440 | tf_op jit(solution)/shard_map/ppermute | solution.py:189
  38.9 18.6 %collective-permute-start.7 = (bf16[32,32,128]{2,1,0:T(8,128)(2,1)S(1)}, bf16[32,32,128]{2,1,0:T(8,128)(2,1)S(1)}, u32[]{:S(2)}, u32[]{:S(2)}) collective-permute-start(bf16[32,32,128]{2,1,0:T(8,128)(2,1)S(1)} %get-tuple-element.20.refs_0_), channel_id=1, source_target_pairs={{0,24},{8,16},{16,8},{24,0},{1,25},{9,17},{17,9},{25,1},{2,26},{10... | collective-permute-start | bytes 786440 | tf_op jit(solution)/shard_map/ppermute | solution.py:189
  54.9 40.2 %collective-permute-start.15 = (bf16[256,32,128]{2,1,0:T(8,128)(2,1)S(1)}, bf16[256,32,128]{2,1,0:T(8,128)(2,1)S(1)}, u32[]{:S(2)}, u32[]{:S(2)}) collective-permute-start(bf16[256,32,128]{2,1,0:T(8,128)(2,1)S(1)} %get-tuple-element.25), channel_id=1, source_target_pairs={{0,1},{1,0},{2,3},{3,2},{4,5},{5,4},{6,7},{7,6},{8,9},{9,8},{10,11... | collective-permute-start | bytes 6291464 | tf_op jit(solution)/shard_map/ppermute | solution.py:201
  56.0 7.8 %collective-permute-start.6 = (bf16[32,32,128]{2,1,0:T(8,128)(2,1)S(1)}, bf16[32,32,128]{2,1,0:T(8,128)(2,1)S(1)}, u32[]{:S(2)}, u32[]{:S(2)}) collective-permute-start(bf16[32,32,128]{2,1,0:T(8,128)(2,1)S(1)} %get-tuple-element.20.refs_0_), channel_id=1, source_target_pairs={{0,8},{8,0},{16,24},{24,16},{1,9},{9,1},{17,25},{25,17},{2,10},{10... | collective-permute-start | bytes 786440 | tf_op jit(solution)/shard_map/ppermute | solution.py:189
  57.5 12.0 %collective-permute-start.8 = (bf16[32,32,128]{2,1,0:T(8,128)(2,1)S(1)}, bf16[32,32,128]{2,1,0:T(8,128)(2,1)S(1)}, u32[]{:S(2)}, u32[]{:S(2)}) collective-permute-start(bf16[32,32,128]{2,1,0:T(8,128)(2,1)S(1)} %collective-permute-done.7.refs_3_), channel_id=1, source_target_pairs={{0,8},{8,0},{16,24},{24,16},{1,9},{9,1},{17,25},{25,17},{2,10},{10... | collective-permute-start | bytes 786440 | tf_op jit(solution)/shard_map/ppermute | solution.py:189
  57.5 19.0 %collective-permute-start.1 = (bf16[32,32,128]{2,1,0:T(8,128)(2,1)S(1)}, bf16[32,32,128]{2,1,0:T(8,128)(2,1)S(1)}, u32[]{:S(2)}, u32[]{:S(2)}) collective-permute-start(bf16[32,32,128]{2,1,0:T(8,128)(2,1)S(1)} %get-tuple-element.17.refs_0_), channel_id=1, source_target_pairs={{0,24},{8,16},{16,8},{24,0},{1,25},{9,17},{17,9},{25,1},{2,26},{10... | collective-permute-start | bytes 786440 | tf_op jit(solution)/shard_map/ppermute | solution.py:189
  73.6 22.1 %collective-permute-start.9 = (bf16[256,32,128]{2,1,0:T(8,128)(2,1)S(1)}, bf16[256,32,128]{2,1,0:T(8,128)(2,1)S(1)}, u32[]{:S(2)}, u32[]{:S(2)}) collective-permute-start(bf16[256,32,128]{2,1,0:T(8,128)(2,1)S(1)} %get-tuple-element.22), channel_id=1, source_target_pairs={{0,1},{1,0},{2,3},{3,2},{4,5},{5,4},{6,7},{7,6},{8,9},{9,8},{10,11... | collective-permute-start | bytes 6291464 | tf_op jit(solution)/shard_map/ppermute | solution.py:201
  74.8 8.4 %collective-permute-start = (bf16[32,32,128]{2,1,0:T(8,128)(2,1)S(1)}, bf16[32,32,128]{2,1,0:T(8,128)(2,1)S(1)}, u32[]{:S(2)}, u32[]{:S(2)}) collective-permute-start(bf16[32,32,128]{2,1,0:T(8,128)(2,1)S(1)} %get-tuple-element.17.refs_0_), channel_id=1, source_target_pairs={{0,8},{8,0},{16,24},{24,16},{1,9},{9,1},{17,25},{25,17},{2,10},{10... | collective-permute-start | bytes 786440 | tf_op jit(solution)/shard_map/ppermute | solution.py:189
  76.5 12.2 %collective-permute-start.2 = (bf16[32,32,128]{2,1,0:T(8,128)(2,1)S(1)}, bf16[32,32,128]{2,1,0:T(8,128)(2,1)S(1)}, u32[]{:S(2)}, u32[]{:S(2)}) collective-permute-start(bf16[32,32,128]{2,1,0:T(8,128)(2,1)S(1)} %collective-permute-done.1.refs_3_), channel_id=1, source_target_pairs={{0,8},{8,0},{16,24},{24,16},{1,9},{9,1},{17,25},{25,17},{2,10},{10... | collective-permute-start | bytes 786440 | tf_op jit(solution)/shard_map/ppermute | solution.py:189
  92.8 4.5 %collective-permute-start.3 = (bf16[256,32,128]{2,1,0:T(8,128)(2,1)S(1)}, bf16[256,32,128]{2,1,0:T(8,128)(2,1)S(1)}, u32[]{:S(2)}, u32[]{:S(2)}) collective-permute-start(bf16[256,32,128]{2,1,0:T(8,128)(2,1)S(1)} %get-tuple-element.19), channel_id=1, source_target_pairs={{0,1},{1,0},{2,3},{3,2},{4,5},{5,4},{6,7},{7,6},{8,9},{9,8},{10,11... | collective-permute-start | bytes 6291464 | tf_op jit(solution)/shard_map/ppermute | solution.py:201
  93.8 24.8 %collective-permute-start.22 = (bf16[128,32,128]{2,1,0:T(8,128)(2,1)S(1)}, bf16[128,32,128]{2,1,0:T(8,128)(2,1)S(1)}, u32[]{:S(2)}, u32[]{:S(2)}) collective-permute-start(bf16[128,32,128]{2,1,0:T(8,128)(2,1)S(1)} %get-tuple-element.30), channel_id=1, source_target_pairs={{0,4},{1,5},{2,6},{3,7},{4,0},{5,1},{6,2},{7,3},{8,12},{9,13},{10,... | collective-permute-start | bytes 3145736 | tf_op jit(solution)/shard_map/ppermute | solution.py:201
  95.3 24.5 %collective-permute-start.16 = (bf16[128,32,128]{2,1,0:T(8,128)(2,1)S(1)}, bf16[128,32,128]{2,1,0:T(8,128)(2,1)S(1)}, u32[]{:S(2)}, u32[]{:S(2)}) collective-permute-start(bf16[128,32,128]{2,1,0:T(8,128)(2,1)S(1)} %get-tuple-element.32), channel_id=1, source_target_pairs={{0,2},{1,3},{2,0},{3,1},{4,6},{5,7},{6,4},{7,5},{8,10},{9,11},{10,... | collective-permute-start | bytes 3145736 | tf_op jit(solution)/shard_map/ppermute | solution.py:201
  95.9 45.2 %collective-permute-start.10 = (bf16[128,32,128]{2,1,0:T(8,128)(2,1)S(1)}, bf16[128,32,128]{2,1,0:T(8,128)(2,1)S(1)}, u32[]{:S(2)}, u32[]{:S(2)}) collective-permute-start(bf16[128,32,128]{2,1,0:T(8,128)(2,1)S(1)} %get-tuple-element.34), channel_id=1, source_target_pairs={{0,4},{1,5},{2,6},{3,7},{4,0},{5,1},{6,2},{7,3},{8,12},{9,13},{10,... | collective-permute-start | bytes 3145736 | tf_op jit(solution)/shard_map/ppermute | solution.py:201
  97.6 44.7 %collective-permute-start.4 = (bf16[128,32,128]{2,1,0:T(8,128)(2,1)S(1)}, bf16[128,32,128]{2,1,0:T(8,128)(2,1)S(1)}, u32[]{:S(2)}, u32[]{:S(2)}) collective-permute-start(bf16[128,32,128]{2,1,0:T(8,128)(2,1)S(1)} %get-tuple-element.36), channel_id=1, source_target_pairs={{0,2},{1,3},{2,0},{3,1},{4,6},{5,7},{6,4},{7,5},{8,10},{9,11},{10,... | collective-permute-start | bytes 3145736 | tf_op jit(solution)/shard_map/ppermute | solution.py:201
  118.6 34.9 %collective-permute-start.23 = (bf16[64,32,128]{2,1,0:T(8,128)(2,1)S(1)}, bf16[64,32,128]{2,1,0:T(8,128)(2,1)S(1)}, u32[]{:S(2)}, u32[]{:S(2)}) collective-permute-start(bf16[64,32,128]{2,1,0:T(8,128)(2,1)S(1)} %get-tuple-element.37), channel_id=1, source_target_pairs={{0,2},{1,3},{2,0},{3,1},{4,6},{5,7},{6,4},{7,5},{8,10},{9,11},{10,... | collective-permute-start | bytes 1572872 | tf_op jit(solution)/shard_map/ppermute | solution.py:201
  119.9 33.6 %collective-permute-start.17 = (bf16[64,32,128]{2,1,0:T(8,128)(2,1)S(1)}, bf16[64,32,128]{2,1,0:T(8,128)(2,1)S(1)}, u32[]{:S(2)}, u32[]{:S(2)}) collective-permute-start(bf16[64,32,128]{2,1,0:T(8,128)(2,1)S(1)} %get-tuple-element.39), channel_id=1, source_target_pairs={{0,4},{1,5},{2,6},{3,7},{4,0},{5,1},{6,2},{7,3},{8,12},{9,13},{10,... | collective-permute-start | bytes 1572872 | tf_op jit(solution)/shard_map/ppermute | solution.py:201
  141.1 23.6 %collective-permute-start.11 = (bf16[64,32,128]{2,1,0:T(8,128)(2,1)S(1)}, bf16[64,32,128]{2,1,0:T(8,128)(2,1)S(1)}, u32[]{:S(2)}, u32[]{:S(2)}) collective-permute-start(bf16[64,32,128]{2,1,0:T(8,128)(2,1)S(1)} %get-tuple-element.41), channel_id=1, source_target_pairs={{0,2},{1,3},{2,0},{3,1},{4,6},{5,7},{6,4},{7,5},{8,10},{9,11},{10,... | collective-permute-start | bytes 1572872 | tf_op jit(solution)/shard_map/ppermute | solution.py:201
  142.4 22.3 %collective-permute-start.5 = (bf16[64,32,128]{2,1,0:T(8,128)(2,1)S(1)}, bf16[64,32,128]{2,1,0:T(8,128)(2,1)S(1)}, u32[]{:S(2)}, u32[]{:S(2)}) collective-permute-start(bf16[64,32,128]{2,1,0:T(8,128)(2,1)S(1)} %get-tuple-element.43), channel_id=1, source_target_pairs={{0,4},{1,5},{2,6},{3,7},{4,0},{5,1},{6,2},{7,3},{8,12},{9,13},{10,... | collective-permute-start | bytes 1572872 | tf_op jit(solution)/shard_map/ppermute | solution.py:201
  (7 other events, 22.9 us)

commit v3 on v2

--- a/solution.py
+++ b/solution.py
@@ -1,3 +1,5 @@
+import functools
+
 import jax
 import jax.numpy as jnp
 from jax import lax
@@ -7,6 +9,7 @@
 
 SLOT_DEV = 64
 MIB = 2**20
+HEIGHTS = (16, 32, 32, 32, 16)
 VMEM = pl.BlockSpec(memory_space=pltpu.VMEM)
 SMEM = pl.BlockSpec(memory_space=pltpu.SMEM)
 
@@ -139,28 +142,30 @@
     )(pos, dst, factor, *parts)
 
 
-def finish_kernel(*refs):
-    *pairs, out_ref = refs
+def finish_kernel(streams, *refs):
+    *arrays, out_ref = refs
     eye = unit(out_ref.shape[1])
     twice = jnp.concatenate([eye, eye], axis=1)
-    for slot in range(out_ref.shape[0]):
-        kept = jnp.concatenate([ref[slot] for ref in pairs[0::2]], axis=0)
-        got = jnp.concatenate([ref[slot] for ref in pairs[1::2]], axis=0)
-        out_ref[slot] = across(twice, jnp.concatenate([kept, got], axis=1), (1, 1))
-
-
-def finish(pairs):
-    slots, _, side = pairs[0][0].shape
-    block = slots // 2
-    flat = [array for pair in pairs for array in pair]
-    return pl.pallas_call(
-        finish_kernel,
-        grid=(slots // block,),
-        in_specs=[
-            pl.BlockSpec((block, array.shape[1], side), lambda i: (i, 0, 0)) for array in flat
-        ],
+    for stream in range(streams):
+
+        @pl.when(pl.program_id(0) == stream)
+        def _(stream=stream):
+            for slot in range(out_ref.shape[0]):
+                kept = jnp.concatenate([ref[slot] for ref in arrays[2 * stream :: 2 * streams]], axis=0)
+                got = jnp.concatenate([ref[slot] for ref in arrays[2 * stream + 1 :: 2 * streams]], axis=0)
+                out_ref[slot] = across(twice, jnp.concatenate([kept, got], axis=1), (1, 1))
+
+
+def finish(chunks):
+    streams = len(chunks[0])
+    block, _, side = chunks[0][0][0].shape
+    flat = [array for chunk in chunks for pair in chunk for array in pair]
+    return pl.pallas_call(
+        functools.partial(finish_kernel, streams),
+        grid=(streams,),
+        in_specs=[VMEM] * len(flat),
         out_specs=pl.BlockSpec((block, side, side), lambda i: (i, 0, 0)),
-        out_shape=jax.ShapeDtypeStruct((slots, side, side), jnp.float32),
+        out_shape=jax.ShapeDtypeStruct((streams * block, side, side), jnp.float32),
         compiler_params=pltpu.CompilerParams(vmem_limit_bytes=16 * MIB),
         name="finish",
     )(*flat)
@@ -173,45 +178,47 @@
     columns, slots = a_cols.T, tile_slot.T
     pos = ((columns // (owners * rows)) ^ plane) * rows + columns % rows
     relative = (slots // SLOT_DEV % owners) ^ me
-    places = []
-    for order in orders:
+    count = len(orders)
+    each = SLOT_DEV // count
+    local = slots % SLOT_DEV
+    dst = jnp.zeros_like(slots)
+    for stream, order in enumerate(orders):
         spot = jnp.zeros_like(relative)
-        for bit in order:
+        for bit in order[1:]:
             spot = spot * 2 + (relative >> bit) % 2
-        places.append(spot * SLOT_DEV + slots % SLOT_DEV)
+        spot = spot * each + local % each + stream * (owners // 2) * each
+        dst = jnp.where(local // each == stream, spot, dst)
+    dst = dst + (relative >> orders[0][0]) % 2 * (owners // 2) * SLOT_DEV
     chunks = turned_chunks(p_vals, heights)
     factor = factors(a_vals, p_vals)
     pairs = []
-    for j, own in enumerate(chunks):
+    for own in chunks:
         got = {0: own}
         for bit in reversed(range(1, planes)):
             relay = planes == 4 and bit == 2
             got[bit] = lax.ppermute(
                 got[3] if relay else own, "grp", flip(planes, 1 if relay else bit)
             )
-        order = orders[j % len(orders)]
         send, keep = partial_sums(
-            pos,
-            places[j % len(orders)],
-            factor,
-            [got[bit] for bit in range(planes)],
-            owners * SLOT_DEV,
+            pos, dst, factor, [got[bit] for bit in range(planes)], owners * SLOT_DEV
         )
-        for at, bit in enumerate(order):
-            back = lax.ppermute(send, "wide", flip(owners, 1 << bit))
-            if at == len(order) - 1:
-                pairs.append((keep, back))
-                break
-            half = keep.shape[0] // 2
-            send, keep = keep[half:] + back[half:], keep[:half] + back[:half]
+        back = lax.ppermute(send, "wide", flip(owners, 1 << orders[0][0]))
+        pairs.append([])
+        for stream, order in enumerate(orders):
+            size = keep.shape[0] // count
+            mine, theirs = (array[stream * size : (stream + 1) * size] for array in (keep, back))
+            for bit in order[1:]:
+                half = mine.shape[0] // 2
+                out, mine = mine[half:] + theirs[half:], mine[:half] + theirs[:half]
+                theirs = lax.ppermute(out, "wide", flip(owners, 1 << bit))
+            pairs[-1].append((mine, theirs))
     return finish(pairs)
 
 
 def solution(mesh):
     owners = mesh.shape["wide"]
     moves = owners.bit_length() - 1
-    height = max(16, min(32, 32 * 8 // owners))
-    heights = (height,) * (128 // height)
+    heights = HEIGHTS if owners <= 8 else (16,) * 8
     orders = [list(range(moves))]
     orders.append([0] + orders[0][:0:-1])
     placed = (

time: 170 us -> 165 us (0.971)
  the two profiles are of different devices: /device:TPU:3 before, /device:TPU:0 now
where the time goes in v3:
time: 165 us
  waiting for transfers between devices  76.5 us (46%)
  starting transfers between devices  54 us (33%)
  Pallas kernels  26 us (16%)
  local copies, waits for them, and re-layouts  5.53 us (3%)
  other arithmetic  2.21 us (1%)
    ppermute x20, waiting for transfers between devices, on_device(): theirs = lax.ppermute(out, 'wide', flip(owners, 1 << bit))  50.9 us
    ppermute x15, starting transfers between devices, on_device(): lax.ppermute(got[3] if relay else own, 'grp', flip(planes, 1 if relay els...  27.6 us
    ppermute x15, waiting for transfers between devices, on_device(): lax.ppermute(got[3] if relay else own, 'grp', flip(planes, 1 if relay els...  25.6 us
    ppermute x20, starting transfers between devices, on_device(): theirs = lax.ppermute(out, 'wide', flip(owners, 1 << bit))  25.5 us
    pallas_call x5, Pallas kernels, partial_sums(): pl.pallas_call(partial_kernel, in_specs=[SMEM, SMEM, VMEM] + [VMEM] * len...  19.5 us
    unnamed x6, local copies, waits for them, and re-layouts  5.53 us
  transfers between devices with their start and end apart: 40, of which 20 were waited for; matrix products, arithmetic and copies ran while one was open for 1% of the time, Pallas kernels for 14%

profile of v3, /device:TPU:0, one launch (start us, length us, event | category | flops | bytes accessed | tf_op | source)
XLA Modules:
  0.0 164.6 jit_solution(15976882528945318286)
XLA Ops:
  2.2 5.1 %collective-permute-start.33 = (bf16[32,16,128]{2,1,0:T(8,128)(2,1)S(1)}, bf16[32,16,128]{2,1,0:T(8,128)(2,1)S(1)}, u32[]{:S(2)}, u32[]{:S(2)}) collective-permute-start(bf16[32,16,128]{2,1,0:T(8,128)(2,1)S(1)} %get-tuple-element.32.refs_0_), channel_id=1, source_target_pairs={{0,24},{8,16},{16,8},{24,0},{1,25},{9,17},{17,9},{25,1},{2,26},{10... | collective-permute-start | bytes 393224 | tf_op jit(solution)/shard_map/ppermute | solution.py:199
  9.4 2.9 %collective-permute-start.25 = (bf16[32,32,128]{2,1,0:T(8,128)(2,1)S(1)}, bf16[32,32,128]{2,1,0:T(8,128)(2,1)S(1)}, u32[]{:S(2)}, u32[]{:S(2)}) collective-permute-start(bf16[32,32,128]{2,1,0:T(8,128)(2,1)S(1)} %get-tuple-element.29.refs_0_), channel_id=1, source_target_pairs={{0,24},{8,16},{16,8},{24,0},{1,25},{9,17},{17,9},{25,1},{2,26},{10... | collective-permute-start | bytes 786440 | tf_op jit(solution)/shard_map/ppermute | solution.py:199
  12.3 2.9 %collective-permute-start.34 = (bf16[32,16,128]{2,1,0:T(8,128)(2,1)S(1)}, bf16[32,16,128]{2,1,0:T(8,128)(2,1)S(1)}, u32[]{:S(2)}, u32[]{:S(2)}) collective-permute-start(bf16[32,16,128]{2,1,0:T(8,128)(2,1)S(1)} %collective-permute-done.33.refs_3_), channel_id=1, source_target_pairs={{0,8},{8,0},{16,24},{24,16},{1,9},{9,1},{17,25},{25,17},{2,10},{10... | collective-permute-start | bytes 393224 | tf_op jit(solution)/shard_map/ppermute | solution.py:199
  17.5 3.1 %copy-done = bf16[32,7,128,128]{3,2,1,0:T(8,128)(2,1)S(1)} copy-done((bf16[32,7,128,128]{3,2,1,0:T(8,128)(2,1)S(1)}, bf16[32,7,128,128]{3,2,1,0:T(8,128)(2,1)}, u32[]{:S(2)}) %copy-start) | copy-done | bytes 7340056
  21.8 2.8 %factors.1.factor_ref = bf16[32,7,128,128]{3,2,1,0:T(8,128)(2,1)S(1)} custom-call(bf16[32,7,128,128]{3,2,1,0:T(8,128)(2,1)S(1)} %copy-done, bf16[32,128,128]{2,1,0:T(8,128)(2,1)S(1)} %copy-done.2), custom_call_target="tpu_custom_call" | custom-call | flops 939524096 | bytes 14680064 | tf_op jit(solution)/shard_map/factors/pallas_call | solution.py:70
  24.5 4.1 %collective-permute-done.34.refs_2_ = bf16[32,16,128]{2,1,0:T(8,128)(2,1)S(1)} collective-permute-done((bf16[32,16,128]{2,1,0:T(8,128)(2,1)S(1)}, bf16[32,16,128]{2,1,0:T(8,128)(2,1)S(1)}, u32[]{:S(2)}, u32[]{:S(2)}) %collective-permute-start.34) | collective-permute-done | bytes 131104 | tf_op jit(solution)/shard_map/ppermute | solution.py:199
  28.6 3.6 %partial.9 = (bf16[256,16,128]{2,1,0:T(8,128)(2,1)S(1)}, bf16[256,16,128]{2,1,0:T(8,128)(2,1)S(1)}) custom-call(s32[7,32]{1,0:T(8,128)S(1)} %get-tuple-element.75.pos_ref, s32[7,32]{1,0:T(8,128)S(1)} %get-tuple-element.76.dst_ref, bf16[32,7,128,128]{3,2,1,0:T(8,128)(2,1)S(1)} %factors.1.factor_ref, bf16[32,16,128]{2,1,0:T(8,128)(2,1)S(1)} %get-tuple-element.32.refs_0_, ...), custom_call_target="tpu_custom_call" | custom-call | flops 117440512 | bytes 9437184 | tf_op jit(solution)/shard_map/partial/pallas_call | solution.py:124
  34.4 2.4 %collective-permute-start.26 = (bf16[32,32,128]{2,1,0:T(8,128)(2,1)S(1)}, bf16[32,32,128]{2,1,0:T(8,128)(2,1)S(1)}, u32[]{:S(2)}, u32[]{:S(2)}) collective-permute-start(bf16[32,32,128]{2,1,0:T(8,128)(2,1)S(1)} %collective-permute-done.25.refs_3_), channel_id=1, source_target_pairs={{0,8},{8,0},{16,24},{24,16},{1,9},{9,1},{17,25},{25,17},{2,10},{10... | collective-permute-start | bytes 786440 | tf_op jit(solution)/shard_map/ppermute | solution.py:199
  36.8 4.7 %collective-permute-start.16 = (bf16[32,32,128]{2,1,0:T(8,128)(2,1)S(1)}, bf16[32,32,128]{2,1,0:T(8,128)(2,1)S(1)}, u32[]{:S(2)}, u32[]{:S(2)}) collective-permute-start(bf16[32,32,128]{2,1,0:T(8,128)(2,1)S(1)} %get-tuple-element.26.refs_0_), channel_id=1, source_target_pairs={{0,8},{8,0},{16,24},{24,16},{1,9},{9,1},{17,25},{25,17},{2,10},{10... | collective-permute-start | bytes 786440 | tf_op jit(solution)/shard_map/ppermute | solution.py:199
  41.5 2.9 %collective-permute-done.2.refs_2_ = bf16[32,16,128]{2,1,0:T(8,128)(2,1)S(1)} collective-permute-done((bf16[32,16,128]{2,1,0:T(8,128)(2,1)S(1)}, bf16[32,16,128]{2,1,0:T(8,128)(2,1)S(1)}, u32[]{:S(2)}, u32[]{:S(2)}) %collective-permute-start.2) | collective-permute-done | bytes 131104 | tf_op jit(solution)/shard_map/ppermute | solution.py:199
  46.3 3.6 %partial.5 = (bf16[256,16,128]{2,1,0:T(8,128)(2,1)S(1)}, bf16[256,16,128]{2,1,0:T(8,128)(2,1)S(1)}) custom-call(s32[7,32]{1,0:T(8,128)S(1)} %get-tuple-element.75.pos_ref, s32[7,32]{1,0:T(8,128)S(1)} %get-tuple-element.76.dst_ref, bf16[32,7,128,128]{3,2,1,0:T(8,128)(2,1)S(1)} %factors.1.factor_ref, bf16[32,16,128]{2,1,0:T(8,128)(2,1)S(1)} %get-tuple-element.20.refs_0_, ...), custom_call_target="tpu_custom_call" | custom-call | flops 117440512 | bytes 9437184 | tf_op jit(solution)/shard_map/partial/pallas_call | solution.py:124
  50.0 4.1 %partial.8 = (bf16[256,32,128]{2,1,0:T(8,128)(2,1)S(1)}, bf16[256,32,128]{2,1,0:T(8,128)(2,1)S(1)}) custom-call(s32[7,32]{1,0:T(8,128)S(1)} %get-tuple-element.75.pos_ref, s32[7,32]{1,0:T(8,128)S(1)} %get-tuple-element.76.dst_ref, bf16[32,7,128,128]{3,2,1,0:T(8,128)(2,1)S(1)} %factors.1.factor_ref, bf16[32,32,128]{2,1,0:T(8,128)(2,1)S(1)} %get-tuple-element.29.refs_0_, ...), custom_call_target="tpu_custom_call" | custom-call | flops 234881024 | bytes 11534336 | tf_op jit(solution)/shard_map/partial/pallas_call | solution.py:124
  56.8 9.5 %collective-permute-done.18.refs_2_ = bf16[32,32,128]{2,1,0:T(8,128)(2,1)S(1)} collective-permute-done((bf16[32,32,128]{2,1,0:T(8,128)(2,1)S(1)}, bf16[32,32,128]{2,1,0:T(8,128)(2,1)S(1)}, u32[]{:S(2)}, u32[]{:S(2)}) %collective-permute-start.18) | collective-permute-done | bytes 262176 | tf_op jit(solution)/shard_map/ppermute | solution.py:199
  66.3 4.1 %partial.7 = (bf16[256,32,128]{2,1,0:T(8,128)(2,1)S(1)}, bf16[256,32,128]{2,1,0:T(8,128)(2,1)S(1)}) custom-call(s32[7,32]{1,0:T(8,128)S(1)} %get-tuple-element.75.pos_ref, s32[7,32]{1,0:T(8,128)S(1)} %get-tuple-element.76.dst_ref, bf16[32,7,128,128]{3,2,1,0:T(8,128)(2,1)S(1)} %factors.1.factor_ref, bf16[32,32,128]{2,1,0:T(8,128)(2,1)S(1)} %get-tuple-element.26.refs_0_, ...), custom_call_target="tpu_custom_call" | custom-call | flops 234881024 | bytes 11534336 | tf_op jit(solution)/shard_map/partial/pallas_call | solution.py:124
  70.4 2.2 %collective-permute-done.8.refs_1_ = bf16[32,32,128]{2,1,0:T(8,128)(2,1)S(1)} collective-permute-done((bf16[32,32,128]{2,1,0:T(8,128)(2,1)S(1)}, bf16[32,32,128]{2,1,0:T(8,128)(2,1)S(1)}, u32[]{:S(2)}, u32[]{:S(2)}) %collective-permute-start.8) | collective-permute-done | bytes 262176 | tf_op jit(solution)/shard_map/ppermute | solution.py:199
  74.0 5.5 %collective-permute-done.10.refs_2_ = bf16[32,32,128]{2,1,0:T(8,128)(2,1)S(1)} collective-permute-done((bf16[32,32,128]{2,1,0:T(8,128)(2,1)S(1)}, bf16[32,32,128]{2,1,0:T(8,128)(2,1)S(1)}, u32[]{:S(2)}, u32[]{:S(2)}) %collective-permute-start.10) | collective-permute-done | bytes 262176 | tf_op jit(solution)/shard_map/ppermute | solution.py:199
  79.4 4.2 %partial.6 = (bf16[256,32,128]{2,1,0:T(8,128)(2,1)S(1)}, bf16[256,32,128]{2,1,0:T(8,128)(2,1)S(1)}) custom-call(s32[7,32]{1,0:T(8,128)S(1)} %get-tuple-element.75.pos_ref, s32[7,32]{1,0:T(8,128)S(1)} %get-tuple-element.76.dst_ref, bf16[32,7,128,128]{3,2,1,0:T(8,128)(2,1)S(1)} %factors.1.factor_ref, bf16[32,32,128]{2,1,0:T(8,128)(2,1)S(1)} %get-tuple-element.23.refs_0_, ...), custom_call_target="tpu_custom_call" | custom-call | flops 234881024 | bytes 11534336 | tf_op jit(solution)/shard_map/partial/pallas_call | solution.py:124
  83.9 2.6 %collective-permute-start.38 = (bf16[64,16,128]{2,1,0:T(8,128)(2,1)S(1)}, bf16[64,16,128]{2,1,0:T(8,128)(2,1)S(1)}, u32[]{:S(2)}, u32[]{:S(2)}) collective-permute-start(bf16[64,16,128]{2,1,0:T(8,128)(2,1)S(1)} %get-tuple-element.48), channel_id=1, source_target_pairs={{0,4},{1,5},{2,6},{3,7},{4,0},{5,1},{6,2},{7,3},{8,12},{9,13},{10,... | collective-permute-start | bytes 786440 | tf_op jit(solution)/shard_map/ppermute | solution.py:213
  88.1 5.4 %collective-permute-done.38 = bf16[64,16,128]{2,1,0:T(8,128)(2,1)S(1)} collective-permute-done((bf16[64,16,128]{2,1,0:T(8,128)(2,1)S(1)}, bf16[64,16,128]{2,1,0:T(8,128)(2,1)S(1)}, u32[]{:S(2)}, u32[]{:S(2)}) %collective-permute-start.38) | collective-permute-done | bytes 262176 | tf_op jit(solution)/shard_map/ppermute | solution.py:213
  96.9 4.7 %collective-permute-done.6 = bf16[64,16,128]{2,1,0:T(8,128)(2,1)S(1)} collective-permute-done((bf16[64,16,128]{2,1,0:T(8,128)(2,1)S(1)}, bf16[64,16,128]{2,1,0:T(8,128)(2,1)S(1)}, u32[]{:S(2)}, u32[]{:S(2)}) %collective-permute-start.6) | collective-permute-done | bytes 262176 | tf_op jit(solution)/shard_map/ppermute | solution.py:213
  108.1 12.6 %collective-permute-done.30 = bf16[64,32,128]{2,1,0:T(8,128)(2,1)S(1)} collective-permute-done((bf16[64,32,128]{2,1,0:T(8,128)(2,1)S(1)}, bf16[64,32,128]{2,1,0:T(8,128)(2,1)S(1)}, u32[]{:S(2)}, u32[]{:S(2)}) %collective-permute-start.30) | collective-permute-done | bytes 524320 | tf_op jit(solution)/shard_map/ppermute | solution.py:213
  123.0 9.0 %collective-permute-done.22 = bf16[64,32,128]{2,1,0:T(8,128)(2,1)S(1)} collective-permute-done((bf16[64,32,128]{2,1,0:T(8,128)(2,1)S(1)}, bf16[64,32,128]{2,1,0:T(8,128)(2,1)S(1)}, u32[]{:S(2)}, u32[]{:S(2)}) %collective-permute-start.22) | collective-permute-done | bytes 524320 | tf_op jit(solution)/shard_map/ppermute | solution.py:213
  134.2 6.7 %collective-permute-done.14 = bf16[64,32,128]{2,1,0:T(8,128)(2,1)S(1)} collective-permute-done((bf16[64,32,128]{2,1,0:T(8,128)(2,1)S(1)}, bf16[64,32,128]{2,1,0:T(8,128)(2,1)S(1)}, u32[]{:S(2)}, u32[]{:S(2)}) %collective-permute-start.14) | collective-permute-done | bytes 524320 | tf_op jit(solution)/shard_map/ppermute | solution.py:213
  161.8 2.8 %finish.1 = f32[64,128,128]{2,1,0:T(8,128)} custom-call(bf16[32,16,128]{2,1,0:T(8,128)(2,1)S(1)} %get-tuple-element.74.refs_0_, bf16[32,16,128]{2,1,0:T(8,128)(2,1)S(1)} %collective-permute-done.5.refs_1_, bf16[32,16,128]{2,1,0:T(8,128)(2,1)S(1)} %get-tuple-element.72.refs_2_, bf16[32,16,128]{2,1,0:T(8,128)(2,1)S(1)} %collective-permute-done.7.refs_3_, ...), custom_call_target="tpu_custom_call" | custom-call | tf_op jit(solution)/shard_map/finish/pallas_call | solution.py:163
  (86 shorter events, 53.1 us)
Async XLA Ops:
  7.4 24.9 %collective-permute-start.1 = (bf16[32,16,128]{2,1,0:T(8,128)(2,1)S(1)}, bf16[32,16,128]{2,1,0:T(8,128)(2,1)S(1)}, u32[]{:S(2)}, u32[]{:S(2)}) collective-permute-start(bf16[32,16,128]{2,1,0:T(8,128)(2,1)S(1)} %get-tuple-element.20.refs_0_), channel_id=1, source_target_pairs={{0,24},{8,16},{16,8},{24,0},{1,25},{9,17},{17,9},{25,1},{2,26},{10... | collective-permute-start | bytes 393224 | tf_op jit(solution)/shard_map/ppermute | solution.py:199
  8.3 26.1 %collective-permute-start = (bf16[32,16,128]{2,1,0:T(8,128)(2,1)S(1)}, bf16[32,16,128]{2,1,0:T(8,128)(2,1)S(1)}, u32[]{:S(2)}, u32[]{:S(2)}) collective-permute-start(bf16[32,16,128]{2,1,0:T(8,128)(2,1)S(1)} %get-tuple-element.20.refs_0_), channel_id=1, source_target_pairs={{0,8},{8,0},{16,24},{24,16},{1,9},{9,1},{17,25},{25,17},{2,10},{10... | collective-permute-start | bytes 393224 | tf_op jit(solution)/shard_map/ppermute | solution.py:199
  9.4 25.0 %collective-permute-start.25 = (bf16[32,32,128]{2,1,0:T(8,128)(2,1)S(1)}, bf16[32,32,128]{2,1,0:T(8,128)(2,1)S(1)}, u32[]{:S(2)}, u32[]{:S(2)}) collective-permute-start(bf16[32,32,128]{2,1,0:T(8,128)(2,1)S(1)} %get-tuple-element.29.refs_0_), channel_id=1, source_target_pairs={{0,24},{8,16},{16,8},{24,0},{1,25},{9,17},{17,9},{25,1},{2,26},{10... | collective-permute-start | bytes 786440 | tf_op jit(solution)/shard_map/ppermute | solution.py:199
  12.3 16.3 %collective-permute-start.34 = (bf16[32,16,128]{2,1,0:T(8,128)(2,1)S(1)}, bf16[32,16,128]{2,1,0:T(8,128)(2,1)S(1)}, u32[]{:S(2)}, u32[]{:S(2)}) collective-permute-start(bf16[32,16,128]{2,1,0:T(8,128)(2,1)S(1)} %collective-permute-done.33.refs_3_), channel_id=1, source_target_pairs={{0,8},{8,0},{16,24},{24,16},{1,9},{9,1},{17,25},{25,17},{2,10},{10... | collective-permute-start | bytes 393224 | tf_op jit(solution)/shard_map/ppermute | solution.py:199
  16.5 20.3 %collective-permute-start.17 = (bf16[32,32,128]{2,1,0:T(8,128)(2,1)S(1)}, bf16[32,32,128]{2,1,0:T(8,128)(2,1)S(1)}, u32[]{:S(2)}, u32[]{:S(2)}) collective-permute-start(bf16[32,32,128]{2,1,0:T(8,128)(2,1)S(1)} %get-tuple-element.26.refs_0_), channel_id=1, source_target_pairs={{0,24},{8,16},{16,8},{24,0},{1,25},{9,17},{17,9},{25,1},{2,26},{10... | collective-permute-start | bytes 786440 | tf_op jit(solution)/shard_map/ppermute | solution.py:199
  32.2 51.6 %collective-permute-start.35 = (bf16[256,16,128]{2,1,0:T(8,128)(2,1)S(1)}, bf16[256,16,128]{2,1,0:T(8,128)(2,1)S(1)}, u32[]{:S(2)}, u32[]{:S(2)}) collective-permute-start(bf16[256,16,128]{2,1,0:T(8,128)(2,1)S(1)} %get-tuple-element.34), channel_id=1, source_target_pairs={{0,1},{1,0},{2,3},{3,2},{4,5},{5,4},{6,7},{7,6},{8,9},{9,8},{10,11... | collective-permute-start | bytes 3145736 | tf_op jit(solution)/shard_map/ppermute | solution.py:205
  32.3 17.6 %collective-permute-start.24 = (bf16[32,32,128]{2,1,0:T(8,128)(2,1)S(1)}, bf16[32,32,128]{2,1,0:T(8,128)(2,1)S(1)}, u32[]{:S(2)}, u32[]{:S(2)}) collective-permute-start(bf16[32,32,128]{2,1,0:T(8,128)(2,1)S(1)} %get-tuple-element.29.refs_0_), channel_id=1, source_target_pairs={{0,8},{8,0},{16,24},{24,16},{1,9},{9,1},{17,25},{25,17},{2,10},{10... | collective-permute-start | bytes 786440 | tf_op jit(solution)/shard_map/ppermute | solution.py:199
  34.4 15.6 %collective-permute-start.26 = (bf16[32,32,128]{2,1,0:T(8,128)(2,1)S(1)}, bf16[32,32,128]{2,1,0:T(8,128)(2,1)S(1)}, u32[]{:S(2)}, u32[]{:S(2)}) collective-permute-start(bf16[32,32,128]{2,1,0:T(8,128)(2,1)S(1)} %collective-permute-done.25.refs_3_), channel_id=1, source_target_pairs={{0,8},{8,0},{16,24},{24,16},{1,9},{9,1},{17,25},{25,17},{2,10},{10... | collective-permute-start | bytes 786440 | tf_op jit(solution)/shard_map/ppermute | solution.py:199
  36.8 18.8 %collective-permute-start.16 = (bf16[32,32,128]{2,1,0:T(8,128)(2,1)S(1)}, bf16[32,32,128]{2,1,0:T(8,128)(2,1)S(1)}, u32[]{:S(2)}, u32[]{:S(2)}) collective-permute-start(bf16[32,32,128]{2,1,0:T(8,128)(2,1)S(1)} %get-tuple-element.26.refs_0_), channel_id=1, source_target_pairs={{0,8},{8,0},{16,24},{24,16},{1,9},{9,1},{17,25},{25,17},{2,10},{10... | collective-permute-start | bytes 786440 | tf_op jit(solution)/shard_map/ppermute | solution.py:199
  44.3 21.9 %collective-permute-start.18 = (bf16[32,32,128]{2,1,0:T(8,128)(2,1)S(1)}, bf16[32,32,128]{2,1,0:T(8,128)(2,1)S(1)}, u32[]{:S(2)}, u32[]{:S(2)}) collective-permute-start(bf16[32,32,128]{2,1,0:T(8,128)(2,1)S(1)} %collective-permute-done.17.refs_3_), channel_id=1, source_target_pairs={{0,8},{8,0},{16,24},{24,16},{1,9},{9,1},{17,25},{25,17},{2,10},{10... | collective-permute-start | bytes 786440 | tf_op jit(solution)/shard_map/ppermute | solution.py:199
  49.9 36.7 %collective-permute-start.3 = (bf16[256,16,128]{2,1,0:T(8,128)(2,1)S(1)}, bf16[256,16,128]{2,1,0:T(8,128)(2,1)S(1)}, u32[]{:S(2)}, u32[]{:S(2)}) collective-permute-start(bf16[256,16,128]{2,1,0:T(8,128)(2,1)S(1)} %get-tuple-element.22), channel_id=1, source_target_pairs={{0,1},{1,0},{2,3},{3,2},{4,5},{5,4},{6,7},{7,6},{8,9},{9,8},{10,11... | collective-permute-start | bytes 3145736 | tf_op jit(solution)/shard_map/ppermute | solution.py:205
  54.1 50.6 %collective-permute-start.27 = (bf16[256,32,128]{2,1,0:T(8,128)(2,1)S(1)}, bf16[256,32,128]{2,1,0:T(8,128)(2,1)S(1)}, u32[]{:S(2)}, u32[]{:S(2)}) collective-permute-start(bf16[256,32,128]{2,1,0:T(8,128)(2,1)S(1)} %get-tuple-element.31), channel_id=1, source_target_pairs={{0,1},{1,0},{2,3},{3,2},{4,5},{5,4},{6,7},{7,6},{8,9},{9,8},{10,11... | collective-permute-start | bytes 6291464 | tf_op jit(solution)/shard_map/ppermute | solution.py:205
  55.6 14.8 %collective-permute-start.9 = (bf16[32,32,128]{2,1,0:T(8,128)(2,1)S(1)}, bf16[32,32,128]{2,1,0:T(8,128)(2,1)S(1)}, u32[]{:S(2)}, u32[]{:S(2)}) collective-permute-start(bf16[32,32,128]{2,1,0:T(8,128)(2,1)S(1)} %get-tuple-element.23.refs_0_), channel_id=1, source_target_pairs={{0,24},{8,16},{16,8},{24,0},{1,25},{9,17},{17,9},{25,1},{2,26},{10... | collective-permute-start | bytes 786440 | tf_op jit(solution)/shard_map/ppermute | solution.py:199
  70.4 35.2 %collective-permute-start.19 = (bf16[256,32,128]{2,1,0:T(8,128)(2,1)S(1)}, bf16[256,32,128]{2,1,0:T(8,128)(2,1)S(1)}, u32[]{:S(2)}, u32[]{:S(2)}) collective-permute-start(bf16[256,32,128]{2,1,0:T(8,128)(2,1)S(1)} %get-tuple-element.28), channel_id=1, source_target_pairs={{0,1},{1,0},{2,3},{3,2},{4,5},{5,4},{6,7},{7,6},{8,9},{9,8},{10,11... | collective-permute-start | bytes 6291464 | tf_op jit(solution)/shard_map/ppermute | solution.py:205
  83.7 23.3 %collective-permute-start.11 = (bf16[256,32,128]{2,1,0:T(8,128)(2,1)S(1)}, bf16[256,32,128]{2,1,0:T(8,128)(2,1)S(1)}, u32[]{:S(2)}, u32[]{:S(2)}) collective-permute-start(bf16[256,32,128]{2,1,0:T(8,128)(2,1)S(1)} %get-tuple-element.25), channel_id=1, source_target_pairs={{0,1},{1,0},{2,3},{3,2},{4,5},{5,4},{6,7},{7,6},{8,9},{9,8},{10,11... | collective-permute-start | bytes 6291464 | tf_op jit(solution)/shard_map/ppermute | solution.py:205
  101.6 44.1 %collective-permute-start.39 = (bf16[32,16,128]{2,1,0:T(8,128)(2,1)S(1)}, bf16[32,16,128]{2,1,0:T(8,128)(2,1)S(1)}, u32[]{:S(2)}, u32[]{:S(2)}) collective-permute-start(bf16[32,16,128]{2,1,0:T(8,128)(2,1)S(1)} %get-tuple-element.67), channel_id=1, source_target_pairs={{0,2},{1,3},{2,0},{3,1},{4,6},{5,7},{6,4},{7,5},{8,10},{9,11},{10,... | collective-permute-start | bytes 393224 | tf_op jit(solution)/shard_map/ppermute | solution.py:213
  103.1 43.2 %collective-permute-start.37 = (bf16[32,16,128]{2,1,0:T(8,128)(2,1)S(1)}, bf16[32,16,128]{2,1,0:T(8,128)(2,1)S(1)}, u32[]{:S(2)}, u32[]{:S(2)}) collective-permute-start(bf16[32,16,128]{2,1,0:T(8,128)(2,1)S(1)} %get-tuple-element.69), channel_id=1, source_target_pairs={{0,4},{1,5},{2,6},{3,7},{4,0},{5,1},{6,2},{7,3},{8,12},{9,13},{10,... | collective-permute-start | bytes 393224 | tf_op jit(solution)/shard_map/ppermute | solution.py:213
  104.9 15.8 %collective-permute-start.30 = (bf16[64,32,128]{2,1,0:T(8,128)(2,1)S(1)}, bf16[64,32,128]{2,1,0:T(8,128)(2,1)S(1)}, u32[]{:S(2)}, u32[]{:S(2)}) collective-permute-start(bf16[64,32,128]{2,1,0:T(8,128)(2,1)S(1)} %get-tuple-element.36), channel_id=1, source_target_pairs={{0,4},{1,5},{2,6},{3,7},{4,0},{5,1},{6,2},{7,3},{8,12},{9,13},{10,... | collective-permute-start | bytes 1572872 | tf_op jit(solution)/shard_map/ppermute | solution.py:213
  105.5 16.6 %collective-permute-start.28 = (bf16[64,32,128]{2,1,0:T(8,128)(2,1)S(1)}, bf16[64,32,128]{2,1,0:T(8,128)(2,1)S(1)}, u32[]{:S(2)}, u32[]{:S(2)}) collective-permute-start(bf16[64,32,128]{2,1,0:T(8,128)(2,1)S(1)} %get-tuple-element.37), channel_id=1, source_target_pairs={{0,2},{1,3},{2,0},{3,1},{4,6},{5,7},{6,4},{7,5},{8,10},{9,11},{10,... | collective-permute-start | bytes 1572872 | tf_op jit(solution)/shard_map/ppermute | solution.py:213
  107.0 25.0 %collective-permute-start.22 = (bf16[64,32,128]{2,1,0:T(8,128)(2,1)S(1)}, bf16[64,32,128]{2,1,0:T(8,128)(2,1)S(1)}, u32[]{:S(2)}, u32[]{:S(2)}) collective-permute-start(bf16[64,32,128]{2,1,0:T(8,128)(2,1)S(1)} %get-tuple-element.40), channel_id=1, source_target_pairs={{0,4},{1,5},{2,6},{3,7},{4,0},{5,1},{6,2},{7,3},{8,12},{9,13},{10,... | collective-permute-start | bytes 1572872 | tf_op jit(solution)/shard_map/ppermute | solution.py:213
  120.8 12.5 %collective-permute-start.20 = (bf16[64,32,128]{2,1,0:T(8,128)(2,1)S(1)}, bf16[64,32,128]{2,1,0:T(8,128)(2,1)S(1)}, u32[]{:S(2)}, u32[]{:S(2)}) collective-permute-start(bf16[64,32,128]{2,1,0:T(8,128)(2,1)S(1)} %get-tuple-element.41), channel_id=1, source_target_pairs={{0,2},{1,3},{2,0},{3,1},{4,6},{5,7},{6,4},{7,5},{8,10},{9,11},{10,... | collective-permute-start | bytes 1572872 | tf_op jit(solution)/shard_map/ppermute | solution.py:213
  122.1 18.8 %collective-permute-start.14 = (bf16[64,32,128]{2,1,0:T(8,128)(2,1)S(1)}, bf16[64,32,128]{2,1,0:T(8,128)(2,1)S(1)}, u32[]{:S(2)}, u32[]{:S(2)}) collective-permute-start(bf16[64,32,128]{2,1,0:T(8,128)(2,1)S(1)} %get-tuple-element.44), channel_id=1, source_target_pairs={{0,4},{1,5},{2,6},{3,7},{4,0},{5,1},{6,2},{7,3},{8,12},{9,13},{10,... | collective-permute-start | bytes 1572872 | tf_op jit(solution)/shard_map/ppermute | solution.py:213
  132.0 12.1 %collective-permute-start.12 = (bf16[64,32,128]{2,1,0:T(8,128)(2,1)S(1)}, bf16[64,32,128]{2,1,0:T(8,128)(2,1)S(1)}, u32[]{:S(2)}, u32[]{:S(2)}) collective-permute-start(bf16[64,32,128]{2,1,0:T(8,128)(2,1)S(1)} %get-tuple-element.45), channel_id=1, source_target_pairs={{0,2},{1,3},{2,0},{3,1},{4,6},{5,7},{6,4},{7,5},{8,10},{9,11},{10,... | collective-permute-start | bytes 1572872 | tf_op jit(solution)/shard_map/ppermute | solution.py:213
  133.3 14.3 %collective-permute-start.7 = (bf16[32,16,128]{2,1,0:T(8,128)(2,1)S(1)}, bf16[32,16,128]{2,1,0:T(8,128)(2,1)S(1)}, u32[]{:S(2)}, u32[]{:S(2)}) collective-permute-start(bf16[32,16,128]{2,1,0:T(8,128)(2,1)S(1)} %get-tuple-element.71), channel_id=1, source_target_pairs={{0,2},{1,3},{2,0},{3,1},{4,6},{5,7},{6,4},{7,5},{8,10},{9,11},{10,... | collective-permute-start | bytes 393224 | tf_op jit(solution)/shard_map/ppermute | solution.py:213
  (19 other events, 153.4 us)

commit v4 on v3

--- a/solution.py
+++ b/solution.py
@@ -146,14 +146,17 @@
     *arrays, out_ref = refs
     eye = unit(out_ref.shape[1])
     twice = jnp.concatenate([eye, eye], axis=1)
-    for stream in range(streams):
-
-        @pl.when(pl.program_id(0) == stream)
-        def _(stream=stream):
-            for slot in range(out_ref.shape[0]):
+    block = out_ref.shape[0]
+    splits = arrays[0].shape[0] // block
+    for step in range(streams * splits):
+
+        @pl.when(pl.program_id(0) == step)
+        def _(stream=step // splits, first=step % splits * block):
+            for at in range(block):
+                slot = first + at
                 kept = jnp.concatenate([ref[slot] for ref in arrays[2 * stream :: 2 * streams]], axis=0)
                 got = jnp.concatenate([ref[slot] for ref in arrays[2 * stream + 1 :: 2 * streams]], axis=0)
-                out_ref[slot] = across(twice, jnp.concatenate([kept, got], axis=1), (1, 1))
+                out_ref[at] = across(twice, jnp.concatenate([kept, got], axis=1), (1, 1))
 
 
 def finish(chunks):
@@ -162,9 +165,9 @@
     flat = [array for chunk in chunks for pair in chunk for array in pair]
     return pl.pallas_call(
         functools.partial(finish_kernel, streams),
-        grid=(streams,),
+        grid=(2 * streams,),
         in_specs=[VMEM] * len(flat),
-        out_specs=pl.BlockSpec((block, side, side), lambda i: (i, 0, 0)),
+        out_specs=pl.BlockSpec((block // 2, side, side), lambda i: (i, 0, 0)),
         out_shape=jax.ShapeDtypeStruct((streams * block, side, side), jnp.float32),
         compiler_params=pltpu.CompilerParams(vmem_limit_bytes=16 * MIB),
         name="finish",

time: 165 us -> 165 us (level)
  transfers between devices with their start and end apart: 40 -> 40, of which waited for: 20 -> 20; matrix products, arithmetic and copies ran while one was open for 1% -> 1% of each run, Pallas kernels for 14% -> 13%
where the time goes in v4:
time: 165 us
  waiting for transfers between devices  76.5 us (46%)
  starting transfers between devices  54 us (33%)
  Pallas kernels  26.6 us (16%)
  local copies, waits for them, and re-layouts  5.53 us (3%)
  other arithmetic  2.21 us (1%)
    ppermute x20, waiting for transfers between devices, on_device(): theirs = lax.ppermute(out, 'wide', flip(owners, 1 << bit))  50.9 us
    ppermute x15, starting transfers between devices, on_device(): lax.ppermute(got[3] if relay else own, 'grp', flip(planes, 1 if relay els...  27.6 us
    ppermute x15, waiting for transfers between devices, on_device(): lax.ppermute(got[3] if relay else own, 'grp', flip(planes, 1 if relay els...  25.6 us
    ppermute x20, starting transfers between devices, on_device(): theirs = lax.ppermute(out, 'wide', flip(owners, 1 << bit))  25.5 us
    pallas_call x5, Pallas kernels, partial_sums(): pl.pallas_call(partial_kernel, in_specs=[SMEM, SMEM, VMEM] + [VMEM] * len...  19.5 us
    unnamed x6, local copies, waits for them, and re-layouts  5.53 us
    pallas_call x1, Pallas kernels, finish(): pl.pallas_call(functools.partial(finish_kernel, streams), grid=(2 * strea...  3.31 us
  transfers between devices with their start and end apart: 40, of which 20 were waited for; matrix products, arithmetic and copies ran while one was open for 1% of the time, Pallas kernels for 13%

profile of v4, /device:TPU:0, one launch (start us, length us, event | category | flops | bytes accessed | tf_op | source)
XLA Modules:
  0.0 165.1 jit_solution(7855938618915704483)
XLA Ops:
  2.2 5.1 %collective-permute-start.33 = (bf16[32,16,128]{2,1,0:T(8,128)(2,1)S(1)}, bf16[32,16,128]{2,1,0:T(8,128)(2,1)S(1)}, u32[]{:S(2)}, u32[]{:S(2)}) collective-permute-start(bf16[32,16,128]{2,1,0:T(8,128)(2,1)S(1)} %get-tuple-element.32.refs_0_), channel_id=1, source_target_pairs={{0,24},{8,16},{16,8},{24,0},{1,25},{9,17},{17,9},{25,1},{2,26},{10... | collective-permute-start | bytes 393224 | tf_op jit(solution)/shard_map/ppermute | solution.py:202
  9.4 2.9 %collective-permute-start.25 = (bf16[32,32,128]{2,1,0:T(8,128)(2,1)S(1)}, bf16[32,32,128]{2,1,0:T(8,128)(2,1)S(1)}, u32[]{:S(2)}, u32[]{:S(2)}) collective-permute-start(bf16[32,32,128]{2,1,0:T(8,128)(2,1)S(1)} %get-tuple-element.29.refs_0_), channel_id=1, source_target_pairs={{0,24},{8,16},{16,8},{24,0},{1,25},{9,17},{17,9},{25,1},{2,26},{10... | collective-permute-start | bytes 786440 | tf_op jit(solution)/shard_map/ppermute | solution.py:202
  12.3 2.9 %collective-permute-start.34 = (bf16[32,16,128]{2,1,0:T(8,128)(2,1)S(1)}, bf16[32,16,128]{2,1,0:T(8,128)(2,1)S(1)}, u32[]{:S(2)}, u32[]{:S(2)}) collective-permute-start(bf16[32,16,128]{2,1,0:T(8,128)(2,1)S(1)} %collective-permute-done.33.refs_3_), channel_id=1, source_target_pairs={{0,8},{8,0},{16,24},{24,16},{1,9},{9,1},{17,25},{25,17},{2,10},{10... | collective-permute-start | bytes 393224 | tf_op jit(solution)/shard_map/ppermute | solution.py:202
  17.5 3.1 %copy-done = bf16[32,7,128,128]{3,2,1,0:T(8,128)(2,1)S(1)} copy-done((bf16[32,7,128,128]{3,2,1,0:T(8,128)(2,1)S(1)}, bf16[32,7,128,128]{3,2,1,0:T(8,128)(2,1)}, u32[]{:S(2)}) %copy-start) | copy-done | bytes 7340056
  21.8 2.8 %factors.1.factor_ref = bf16[32,7,128,128]{3,2,1,0:T(8,128)(2,1)S(1)} custom-call(bf16[32,7,128,128]{3,2,1,0:T(8,128)(2,1)S(1)} %copy-done, bf16[32,128,128]{2,1,0:T(8,128)(2,1)S(1)} %copy-done.2), custom_call_target="tpu_custom_call" | custom-call | flops 939524096 | bytes 14680064 | tf_op jit(solution)/shard_map/factors/pallas_call | solution.py:70
  24.5 4.1 %collective-permute-done.34.refs_2_ = bf16[32,16,128]{2,1,0:T(8,128)(2,1)S(1)} collective-permute-done((bf16[32,16,128]{2,1,0:T(8,128)(2,1)S(1)}, bf16[32,16,128]{2,1,0:T(8,128)(2,1)S(1)}, u32[]{:S(2)}, u32[]{:S(2)}) %collective-permute-start.34) | collective-permute-done | bytes 131104 | tf_op jit(solution)/shard_map/ppermute | solution.py:202
  28.6 3.6 %partial.9 = (bf16[256,16,128]{2,1,0:T(8,128)(2,1)S(1)}, bf16[256,16,128]{2,1,0:T(8,128)(2,1)S(1)}) custom-call(s32[7,32]{1,0:T(8,128)S(1)} %get-tuple-element.75.pos_ref, s32[7,32]{1,0:T(8,128)S(1)} %get-tuple-element.76.dst_ref, bf16[32,7,128,128]{3,2,1,0:T(8,128)(2,1)S(1)} %factors.1.factor_ref, bf16[32,16,128]{2,1,0:T(8,128)(2,1)S(1)} %get-tuple-element.32.refs_0_, ...), custom_call_target="tpu_custom_call" | custom-call | flops 117440512 | bytes 9437184 | tf_op jit(solution)/shard_map/partial/pallas_call | solution.py:124
  34.4 2.4 %collective-permute-start.26 = (bf16[32,32,128]{2,1,0:T(8,128)(2,1)S(1)}, bf16[32,32,128]{2,1,0:T(8,128)(2,1)S(1)}, u32[]{:S(2)}, u32[]{:S(2)}) collective-permute-start(bf16[32,32,128]{2,1,0:T(8,128)(2,1)S(1)} %collective-permute-done.25.refs_3_), channel_id=1, source_target_pairs={{0,8},{8,0},{16,24},{24,16},{1,9},{9,1},{17,25},{25,17},{2,10},{10... | collective-permute-start | bytes 786440 | tf_op jit(solution)/shard_map/ppermute | solution.py:202
  36.8 4.7 %collective-permute-start.16 = (bf16[32,32,128]{2,1,0:T(8,128)(2,1)S(1)}, bf16[32,32,128]{2,1,0:T(8,128)(2,1)S(1)}, u32[]{:S(2)}, u32[]{:S(2)}) collective-permute-start(bf16[32,32,128]{2,1,0:T(8,128)(2,1)S(1)} %get-tuple-element.26.refs_0_), channel_id=1, source_target_pairs={{0,8},{8,0},{16,24},{24,16},{1,9},{9,1},{17,25},{25,17},{2,10},{10... | collective-permute-start | bytes 786440 | tf_op jit(solution)/shard_map/ppermute | solution.py:202
  41.5 2.9 %collective-permute-done.2.refs_2_ = bf16[32,16,128]{2,1,0:T(8,128)(2,1)S(1)} collective-permute-done((bf16[32,16,128]{2,1,0:T(8,128)(2,1)S(1)}, bf16[32,16,128]{2,1,0:T(8,128)(2,1)S(1)}, u32[]{:S(2)}, u32[]{:S(2)}) %collective-permute-start.2) | collective-permute-done | bytes 131104 | tf_op jit(solution)/shard_map/ppermute | solution.py:202
  46.3 3.6 %partial.5 = (bf16[256,16,128]{2,1,0:T(8,128)(2,1)S(1)}, bf16[256,16,128]{2,1,0:T(8,128)(2,1)S(1)}) custom-call(s32[7,32]{1,0:T(8,128)S(1)} %get-tuple-element.75.pos_ref, s32[7,32]{1,0:T(8,128)S(1)} %get-tuple-element.76.dst_ref, bf16[32,7,128,128]{3,2,1,0:T(8,128)(2,1)S(1)} %factors.1.factor_ref, bf16[32,16,128]{2,1,0:T(8,128)(2,1)S(1)} %get-tuple-element.20.refs_0_, ...), custom_call_target="tpu_custom_call" | custom-call | flops 117440512 | bytes 9437184 | tf_op jit(solution)/shard_map/partial/pallas_call | solution.py:124
  50.0 4.1 %partial.8 = (bf16[256,32,128]{2,1,0:T(8,128)(2,1)S(1)}, bf16[256,32,128]{2,1,0:T(8,128)(2,1)S(1)}) custom-call(s32[7,32]{1,0:T(8,128)S(1)} %get-tuple-element.75.pos_ref, s32[7,32]{1,0:T(8,128)S(1)} %get-tuple-element.76.dst_ref, bf16[32,7,128,128]{3,2,1,0:T(8,128)(2,1)S(1)} %factors.1.factor_ref, bf16[32,32,128]{2,1,0:T(8,128)(2,1)S(1)} %get-tuple-element.29.refs_0_, ...), custom_call_target="tpu_custom_call" | custom-call | flops 234881024 | bytes 11534336 | tf_op jit(solution)/shard_map/partial/pallas_call | solution.py:124
  56.8 9.5 %collective-permute-done.18.refs_2_ = bf16[32,32,128]{2,1,0:T(8,128)(2,1)S(1)} collective-permute-done((bf16[32,32,128]{2,1,0:T(8,128)(2,1)S(1)}, bf16[32,32,128]{2,1,0:T(8,128)(2,1)S(1)}, u32[]{:S(2)}, u32[]{:S(2)}) %collective-permute-start.18) | collective-permute-done | bytes 262176 | tf_op jit(solution)/shard_map/ppermute | solution.py:202
  66.3 4.1 %partial.7 = (bf16[256,32,128]{2,1,0:T(8,128)(2,1)S(1)}, bf16[256,32,128]{2,1,0:T(8,128)(2,1)S(1)}) custom-call(s32[7,32]{1,0:T(8,128)S(1)} %get-tuple-element.75.pos_ref, s32[7,32]{1,0:T(8,128)S(1)} %get-tuple-element.76.dst_ref, bf16[32,7,128,128]{3,2,1,0:T(8,128)(2,1)S(1)} %factors.1.factor_ref, bf16[32,32,128]{2,1,0:T(8,128)(2,1)S(1)} %get-tuple-element.26.refs_0_, ...), custom_call_target="tpu_custom_call" | custom-call | flops 234881024 | bytes 11534336 | tf_op jit(solution)/shard_map/partial/pallas_call | solution.py:124
  70.4 2.2 %collective-permute-done.8.refs_1_ = bf16[32,32,128]{2,1,0:T(8,128)(2,1)S(1)} collective-permute-done((bf16[32,32,128]{2,1,0:T(8,128)(2,1)S(1)}, bf16[32,32,128]{2,1,0:T(8,128)(2,1)S(1)}, u32[]{:S(2)}, u32[]{:S(2)}) %collective-permute-start.8) | collective-permute-done | bytes 262176 | tf_op jit(solution)/shard_map/ppermute | solution.py:202
  74.0 5.5 %collective-permute-done.10.refs_2_ = bf16[32,32,128]{2,1,0:T(8,128)(2,1)S(1)} collective-permute-done((bf16[32,32,128]{2,1,0:T(8,128)(2,1)S(1)}, bf16[32,32,128]{2,1,0:T(8,128)(2,1)S(1)}, u32[]{:S(2)}, u32[]{:S(2)}) %collective-permute-start.10) | collective-permute-done | bytes 262176 | tf_op jit(solution)/shard_map/ppermute | solution.py:202
  79.4 4.2 %partial.6 = (bf16[256,32,128]{2,1,0:T(8,128)(2,1)S(1)}, bf16[256,32,128]{2,1,0:T(8,128)(2,1)S(1)}) custom-call(s32[7,32]{1,0:T(8,128)S(1)} %get-tuple-element.75.pos_ref, s32[7,32]{1,0:T(8,128)S(1)} %get-tuple-element.76.dst_ref, bf16[32,7,128,128]{3,2,1,0:T(8,128)(2,1)S(1)} %factors.1.factor_ref, bf16[32,32,128]{2,1,0:T(8,128)(2,1)S(1)} %get-tuple-element.23.refs_0_, ...), custom_call_target="tpu_custom_call" | custom-call | flops 234881024 | bytes 11534336 | tf_op jit(solution)/shard_map/partial/pallas_call | solution.py:124
  83.9 2.6 %collective-permute-start.38 = (bf16[64,16,128]{2,1,0:T(8,128)(2,1)S(1)}, bf16[64,16,128]{2,1,0:T(8,128)(2,1)S(1)}, u32[]{:S(2)}, u32[]{:S(2)}) collective-permute-start(bf16[64,16,128]{2,1,0:T(8,128)(2,1)S(1)} %get-tuple-element.48), channel_id=1, source_target_pairs={{0,4},{1,5},{2,6},{3,7},{4,0},{5,1},{6,2},{7,3},{8,12},{9,13},{10,... | collective-permute-start | bytes 786440 | tf_op jit(solution)/shard_map/ppermute | solution.py:216
  88.1 5.4 %collective-permute-done.38 = bf16[64,16,128]{2,1,0:T(8,128)(2,1)S(1)} collective-permute-done((bf16[64,16,128]{2,1,0:T(8,128)(2,1)S(1)}, bf16[64,16,128]{2,1,0:T(8,128)(2,1)S(1)}, u32[]{:S(2)}, u32[]{:S(2)}) %collective-permute-start.38) | collective-permute-done | bytes 262176 | tf_op jit(solution)/shard_map/ppermute | solution.py:216
  96.9 4.7 %collective-permute-done.6 = bf16[64,16,128]{2,1,0:T(8,128)(2,1)S(1)} collective-permute-done((bf16[64,16,128]{2,1,0:T(8,128)(2,1)S(1)}, bf16[64,16,128]{2,1,0:T(8,128)(2,1)S(1)}, u32[]{:S(2)}, u32[]{:S(2)}) %collective-permute-start.6) | collective-permute-done | bytes 262176 | tf_op jit(solution)/shard_map/ppermute | solution.py:216
  108.1 12.6 %collective-permute-done.30 = bf16[64,32,128]{2,1,0:T(8,128)(2,1)S(1)} collective-permute-done((bf16[64,32,128]{2,1,0:T(8,128)(2,1)S(1)}, bf16[64,32,128]{2,1,0:T(8,128)(2,1)S(1)}, u32[]{:S(2)}, u32[]{:S(2)}) %collective-permute-start.30) | collective-permute-done | bytes 524320 | tf_op jit(solution)/shard_map/ppermute | solution.py:216
  123.0 9.0 %collective-permute-done.22 = bf16[64,32,128]{2,1,0:T(8,128)(2,1)S(1)} collective-permute-done((bf16[64,32,128]{2,1,0:T(8,128)(2,1)S(1)}, bf16[64,32,128]{2,1,0:T(8,128)(2,1)S(1)}, u32[]{:S(2)}, u32[]{:S(2)}) %collective-permute-start.22) | collective-permute-done | bytes 524320 | tf_op jit(solution)/shard_map/ppermute | solution.py:216
  134.2 6.7 %collective-permute-done.14 = bf16[64,32,128]{2,1,0:T(8,128)(2,1)S(1)} collective-permute-done((bf16[64,32,128]{2,1,0:T(8,128)(2,1)S(1)}, bf16[64,32,128]{2,1,0:T(8,128)(2,1)S(1)}, u32[]{:S(2)}, u32[]{:S(2)}) %collective-permute-start.14) | collective-permute-done | bytes 524320 | tf_op jit(solution)/shard_map/ppermute | solution.py:216
  161.8 3.3 %finish.1 = f32[64,128,128]{2,1,0:T(8,128)} custom-call(bf16[32,16,128]{2,1,0:T(8,128)(2,1)S(1)} %get-tuple-element.74.refs_0_, bf16[32,16,128]{2,1,0:T(8,128)(2,1)S(1)} %collective-permute-done.5.refs_1_, bf16[32,16,128]{2,1,0:T(8,128)(2,1)S(1)} %get-tuple-element.72.refs_2_, bf16[32,16,128]{2,1,0:T(8,128)(2,1)S(1)} %collective-permute-done.7.refs_3_, ...), custom_call_target="tpu_custom_call" | custom-call | tf_op jit(solution)/shard_map/finish/pallas_call | solution.py:166
  (86 shorter events, 53.1 us)
Async XLA Ops:
  7.4 24.9 %collective-permute-start.1 = (bf16[32,16,128]{2,1,0:T(8,128)(2,1)S(1)}, bf16[32,16,128]{2,1,0:T(8,128)(2,1)S(1)}, u32[]{:S(2)}, u32[]{:S(2)}) collective-permute-start(bf16[32,16,128]{2,1,0:T(8,128)(2,1)S(1)} %get-tuple-element.20.refs_0_), channel_id=1, source_target_pairs={{0,24},{8,16},{16,8},{24,0},{1,25},{9,17},{17,9},{25,1},{2,26},{10... | collective-permute-start | bytes 393224 | tf_op jit(solution)/shard_map/ppermute | solution.py:202
  8.3 26.1 %collective-permute-start = (bf16[32,16,128]{2,1,0:T(8,128)(2,1)S(1)}, bf16[32,16,128]{2,1,0:T(8,128)(2,1)S(1)}, u32[]{:S(2)}, u32[]{:S(2)}) collective-permute-start(bf16[32,16,128]{2,1,0:T(8,128)(2,1)S(1)} %get-tuple-element.20.refs_0_), channel_id=1, source_target_pairs={{0,8},{8,0},{16,24},{24,16},{1,9},{9,1},{17,25},{25,17},{2,10},{10... | collective-permute-start | bytes 393224 | tf_op jit(solution)/shard_map/ppermute | solution.py:202
  9.4 25.0 %collective-permute-start.25 = (bf16[32,32,128]{2,1,0:T(8,128)(2,1)S(1)}, bf16[32,32,128]{2,1,0:T(8,128)(2,1)S(1)}, u32[]{:S(2)}, u32[]{:S(2)}) collective-permute-start(bf16[32,32,128]{2,1,0:T(8,128)(2,1)S(1)} %get-tuple-element.29.refs_0_), channel_id=1, source_target_pairs={{0,24},{8,16},{16,8},{24,0},{1,25},{9,17},{17,9},{25,1},{2,26},{10... | collective-permute-start | bytes 786440 | tf_op jit(solution)/shard_map/ppermute | solution.py:202
  12.3 16.3 %collective-permute-start.34 = (bf16[32,16,128]{2,1,0:T(8,128)(2,1)S(1)}, bf16[32,16,128]{2,1,0:T(8,128)(2,1)S(1)}, u32[]{:S(2)}, u32[]{:S(2)}) collective-permute-start(bf16[32,16,128]{2,1,0:T(8,128)(2,1)S(1)} %collective-permute-done.33.refs_3_), channel_id=1, source_target_pairs={{0,8},{8,0},{16,24},{24,16},{1,9},{9,1},{17,25},{25,17},{2,10},{10... | collective-permute-start | bytes 393224 | tf_op jit(solution)/shard_map/ppermute | solution.py:202
  16.5 20.3 %collective-permute-start.17 = (bf16[32,32,128]{2,1,0:T(8,128)(2,1)S(1)}, bf16[32,32,128]{2,1,0:T(8,128)(2,1)S(1)}, u32[]{:S(2)}, u32[]{:S(2)}) collective-permute-start(bf16[32,32,128]{2,1,0:T(8,128)(2,1)S(1)} %get-tuple-element.26.refs_0_), channel_id=1, source_target_pairs={{0,24},{8,16},{16,8},{24,0},{1,25},{9,17},{17,9},{25,1},{2,26},{10... | collective-permute-start | bytes 786440 | tf_op jit(solution)/shard_map/ppermute | solution.py:202
  32.2 51.6 %collective-permute-start.35 = (bf16[256,16,128]{2,1,0:T(8,128)(2,1)S(1)}, bf16[256,16,128]{2,1,0:T(8,128)(2,1)S(1)}, u32[]{:S(2)}, u32[]{:S(2)}) collective-permute-start(bf16[256,16,128]{2,1,0:T(8,128)(2,1)S(1)} %get-tuple-element.34), channel_id=1, source_target_pairs={{0,1},{1,0},{2,3},{3,2},{4,5},{5,4},{6,7},{7,6},{8,9},{9,8},{10,11... | collective-permute-start | bytes 3145736 | tf_op jit(solution)/shard_map/ppermute | solution.py:208
  32.3 17.6 %collective-permute-start.24 = (bf16[32,32,128]{2,1,0:T(8,128)(2,1)S(1)}, bf16[32,32,128]{2,1,0:T(8,128)(2,1)S(1)}, u32[]{:S(2)}, u32[]{:S(2)}) collective-permute-start(bf16[32,32,128]{2,1,0:T(8,128)(2,1)S(1)} %get-tuple-element.29.refs_0_), channel_id=1, source_target_pairs={{0,8},{8,0},{16,24},{24,16},{1,9},{9,1},{17,25},{25,17},{2,10},{10... | collective-permute-start | bytes 786440 | tf_op jit(solution)/shard_map/ppermute | solution.py:202
  34.4 15.6 %collective-permute-start.26 = (bf16[32,32,128]{2,1,0:T(8,128)(2,1)S(1)}, bf16[32,32,128]{2,1,0:T(8,128)(2,1)S(1)}, u32[]{:S(2)}, u32[]{:S(2)}) collective-permute-start(bf16[32,32,128]{2,1,0:T(8,128)(2,1)S(1)} %collective-permute-done.25.refs_3_), channel_id=1, source_target_pairs={{0,8},{8,0},{16,24},{24,16},{1,9},{9,1},{17,25},{25,17},{2,10},{10... | collective-permute-start | bytes 786440 | tf_op jit(solution)/shard_map/ppermute | solution.py:202
  36.8 18.8 %collective-permute-start.16 = (bf16[32,32,128]{2,1,0:T(8,128)(2,1)S(1)}, bf16[32,32,128]{2,1,0:T(8,128)(2,1)S(1)}, u32[]{:S(2)}, u32[]{:S(2)}) collective-permute-start(bf16[32,32,128]{2,1,0:T(8,128)(2,1)S(1)} %get-tuple-element.26.refs_0_), channel_id=1, source_target_pairs={{0,8},{8,0},{16,24},{24,16},{1,9},{9,1},{17,25},{25,17},{2,10},{10... | collective-permute-start | bytes 786440 | tf_op jit(solution)/shard_map/ppermute | solution.py:202
  44.3 21.9 %collective-permute-start.18 = (bf16[32,32,128]{2,1,0:T(8,128)(2,1)S(1)}, bf16[32,32,128]{2,1,0:T(8,128)(2,1)S(1)}, u32[]{:S(2)}, u32[]{:S(2)}) collective-permute-start(bf16[32,32,128]{2,1,0:T(8,128)(2,1)S(1)} %collective-permute-done.17.refs_3_), channel_id=1, source_target_pairs={{0,8},{8,0},{16,24},{24,16},{1,9},{9,1},{17,25},{25,17},{2,10},{10... | collective-permute-start | bytes 786440 | tf_op jit(solution)/shard_map/ppermute | solution.py:202
  49.9 36.7 %collective-permute-start.3 = (bf16[256,16,128]{2,1,0:T(8,128)(2,1)S(1)}, bf16[256,16,128]{2,1,0:T(8,128)(2,1)S(1)}, u32[]{:S(2)}, u32[]{:S(2)}) collective-permute-start(bf16[256,16,128]{2,1,0:T(8,128)(2,1)S(1)} %get-tuple-element.22), channel_id=1, source_target_pairs={{0,1},{1,0},{2,3},{3,2},{4,5},{5,4},{6,7},{7,6},{8,9},{9,8},{10,11... | collective-permute-start | bytes 3145736 | tf_op jit(solution)/shard_map/ppermute | solution.py:208
  54.1 50.6 %collective-permute-start.27 = (bf16[256,32,128]{2,1,0:T(8,128)(2,1)S(1)}, bf16[256,32,128]{2,1,0:T(8,128)(2,1)S(1)}, u32[]{:S(2)}, u32[]{:S(2)}) collective-permute-start(bf16[256,32,128]{2,1,0:T(8,128)(2,1)S(1)} %get-tuple-element.31), channel_id=1, source_target_pairs={{0,1},{1,0},{2,3},{3,2},{4,5},{5,4},{6,7},{7,6},{8,9},{9,8},{10,11... | collective-permute-start | bytes 6291464 | tf_op jit(solution)/shard_map/ppermute | solution.py:208
  55.6 14.8 %collective-permute-start.9 = (bf16[32,32,128]{2,1,0:T(8,128)(2,1)S(1)}, bf16[32,32,128]{2,1,0:T(8,128)(2,1)S(1)}, u32[]{:S(2)}, u32[]{:S(2)}) collective-permute-start(bf16[32,32,128]{2,1,0:T(8,128)(2,1)S(1)} %get-tuple-element.23.refs_0_), channel_id=1, source_target_pairs={{0,24},{8,16},{16,8},{24,0},{1,25},{9,17},{17,9},{25,1},{2,26},{10... | collective-permute-start | bytes 786440 | tf_op jit(solution)/shard_map/ppermute | solution.py:202
  70.4 35.2 %collective-permute-start.19 = (bf16[256,32,128]{2,1,0:T(8,128)(2,1)S(1)}, bf16[256,32,128]{2,1,0:T(8,128)(2,1)S(1)}, u32[]{:S(2)}, u32[]{:S(2)}) collective-permute-start(bf16[256,32,128]{2,1,0:T(8,128)(2,1)S(1)} %get-tuple-element.28), channel_id=1, source_target_pairs={{0,1},{1,0},{2,3},{3,2},{4,5},{5,4},{6,7},{7,6},{8,9},{9,8},{10,11... | collective-permute-start | bytes 6291464 | tf_op jit(solution)/shard_map/ppermute | solution.py:208
  83.7 23.3 %collective-permute-start.11 = (bf16[256,32,128]{2,1,0:T(8,128)(2,1)S(1)}, bf16[256,32,128]{2,1,0:T(8,128)(2,1)S(1)}, u32[]{:S(2)}, u32[]{:S(2)}) collective-permute-start(bf16[256,32,128]{2,1,0:T(8,128)(2,1)S(1)} %get-tuple-element.25), channel_id=1, source_target_pairs={{0,1},{1,0},{2,3},{3,2},{4,5},{5,4},{6,7},{7,6},{8,9},{9,8},{10,11... | collective-permute-start | bytes 6291464 | tf_op jit(solution)/shard_map/ppermute | solution.py:208
  101.6 44.1 %collective-permute-start.39 = (bf16[32,16,128]{2,1,0:T(8,128)(2,1)S(1)}, bf16[32,16,128]{2,1,0:T(8,128)(2,1)S(1)}, u32[]{:S(2)}, u32[]{:S(2)}) collective-permute-start(bf16[32,16,128]{2,1,0:T(8,128)(2,1)S(1)} %get-tuple-element.67), channel_id=1, source_target_pairs={{0,2},{1,3},{2,0},{3,1},{4,6},{5,7},{6,4},{7,5},{8,10},{9,11},{10,... | collective-permute-start | bytes 393224 | tf_op jit(solution)/shard_map/ppermute | solution.py:216
  103.1 43.2 %collective-permute-start.37 = (bf16[32,16,128]{2,1,0:T(8,128)(2,1)S(1)}, bf16[32,16,128]{2,1,0:T(8,128)(2,1)S(1)}, u32[]{:S(2)}, u32[]{:S(2)}) collective-permute-start(bf16[32,16,128]{2,1,0:T(8,128)(2,1)S(1)} %get-tuple-element.69), channel_id=1, source_target_pairs={{0,4},{1,5},{2,6},{3,7},{4,0},{5,1},{6,2},{7,3},{8,12},{9,13},{10,... | collective-permute-start | bytes 393224 | tf_op jit(solution)/shard_map/ppermute | solution.py:216
  104.9 15.8 %collective-permute-start.30 = (bf16[64,32,128]{2,1,0:T(8,128)(2,1)S(1)}, bf16[64,32,128]{2,1,0:T(8,128)(2,1)S(1)}, u32[]{:S(2)}, u32[]{:S(2)}) collective-permute-start(bf16[64,32,128]{2,1,0:T(8,128)(2,1)S(1)} %get-tuple-element.36), channel_id=1, source_target_pairs={{0,4},{1,5},{2,6},{3,7},{4,0},{5,1},{6,2},{7,3},{8,12},{9,13},{10,... | collective-permute-start | bytes 1572872 | tf_op jit(solution)/shard_map/ppermute | solution.py:216
  105.5 16.6 %collective-permute-start.28 = (bf16[64,32,128]{2,1,0:T(8,128)(2,1)S(1)}, bf16[64,32,128]{2,1,0:T(8,128)(2,1)S(1)}, u32[]{:S(2)}, u32[]{:S(2)}) collective-permute-start(bf16[64,32,128]{2,1,0:T(8,128)(2,1)S(1)} %get-tuple-element.37), channel_id=1, source_target_pairs={{0,2},{1,3},{2,0},{3,1},{4,6},{5,7},{6,4},{7,5},{8,10},{9,11},{10,... | collective-permute-start | bytes 1572872 | tf_op jit(solution)/shard_map/ppermute | solution.py:216
  107.0 25.0 %collective-permute-start.22 = (bf16[64,32,128]{2,1,0:T(8,128)(2,1)S(1)}, bf16[64,32,128]{2,1,0:T(8,128)(2,1)S(1)}, u32[]{:S(2)}, u32[]{:S(2)}) collective-permute-start(bf16[64,32,128]{2,1,0:T(8,128)(2,1)S(1)} %get-tuple-element.40), channel_id=1, source_target_pairs={{0,4},{1,5},{2,6},{3,7},{4,0},{5,1},{6,2},{7,3},{8,12},{9,13},{10,... | collective-permute-start | bytes 1572872 | tf_op jit(solution)/shard_map/ppermute | solution.py:216
  120.8 12.5 %collective-permute-start.20 = (bf16[64,32,128]{2,1,0:T(8,128)(2,1)S(1)}, bf16[64,32,128]{2,1,0:T(8,128)(2,1)S(1)}, u32[]{:S(2)}, u32[]{:S(2)}) collective-permute-start(bf16[64,32,128]{2,1,0:T(8,128)(2,1)S(1)} %get-tuple-element.41), channel_id=1, source_target_pairs={{0,2},{1,3},{2,0},{3,1},{4,6},{5,7},{6,4},{7,5},{8,10},{9,11},{10,... | collective-permute-start | bytes 1572872 | tf_op jit(solution)/shard_map/ppermute | solution.py:216
  122.1 18.8 %collective-permute-start.14 = (bf16[64,32,128]{2,1,0:T(8,128)(2,1)S(1)}, bf16[64,32,128]{2,1,0:T(8,128)(2,1)S(1)}, u32[]{:S(2)}, u32[]{:S(2)}) collective-permute-start(bf16[64,32,128]{2,1,0:T(8,128)(2,1)S(1)} %get-tuple-element.44), channel_id=1, source_target_pairs={{0,4},{1,5},{2,6},{3,7},{4,0},{5,1},{6,2},{7,3},{8,12},{9,13},{10,... | collective-permute-start | bytes 1572872 | tf_op jit(solution)/shard_map/ppermute | solution.py:216
  132.0 12.1 %collective-permute-start.12 = (bf16[64,32,128]{2,1,0:T(8,128)(2,1)S(1)}, bf16[64,32,128]{2,1,0:T(8,128)(2,1)S(1)}, u32[]{:S(2)}, u32[]{:S(2)}) collective-permute-start(bf16[64,32,128]{2,1,0:T(8,128)(2,1)S(1)} %get-tuple-element.45), channel_id=1, source_target_pairs={{0,2},{1,3},{2,0},{3,1},{4,6},{5,7},{6,4},{7,5},{8,10},{9,11},{10,... | collective-permute-start | bytes 1572872 | tf_op jit(solution)/shard_map/ppermute | solution.py:216
  133.3 14.3 %collective-permute-start.7 = (bf16[32,16,128]{2,1,0:T(8,128)(2,1)S(1)}, bf16[32,16,128]{2,1,0:T(8,128)(2,1)S(1)}, u32[]{:S(2)}, u32[]{:S(2)}) collective-permute-start(bf16[32,16,128]{2,1,0:T(8,128)(2,1)S(1)} %get-tuple-element.71), channel_id=1, source_target_pairs={{0,2},{1,3},{2,0},{3,1},{4,6},{5,7},{6,4},{7,5},{8,10},{9,11},{10,... | collective-permute-start | bytes 393224 | tf_op jit(solution)/shard_map/ppermute | solution.py:216
  (19 other events, 153.4 us)
